TPU v7x, 32 devices: a whole 2x2x4 slice. The times are simulated.
32 devices in a mesh: groups: 2 (over x), ctx: 16 (over z, y, core).
Axes of the slice: x: 2, y: 2, z: 4, core: 2. Of those that a mesh axis runs over, the one named last changes fastest.
Arguments:
- q_latent: bfloat16 [128, 1536], P(('groups', 'ctx')), parts along dimension 0, may hold values from -64 to 64
- q_gain: float32 [1536], replicated, may hold values from 0.1 to 1.9
- w_uq: bfloat16 [1536, 24576], P(None, 'ctx'), may hold values from -0.15625 to 0.15625
- w_uk: bfloat16 [128, 128, 512], P('ctx'), may hold values from -0.5 to 0.5
- w_uv: bfloat16 [128, 512, 128], P('ctx'), may hold values from -0.25 to 0.25
- w_o: bfloat16 [16384, 7168], P('ctx'), may hold values from -0.046875 to 0.046875
- latent_cache: bfloat16 [65536, 576], P(('groups', 'ctx')), parts along dimension 0, may hold values from -1024 to 1024
- kv_scales: float32 [65536, 4], P(('groups', 'ctx')), parts along dimension 0, may hold values from 0.5 to 2
- selected: int32 [128, 32], P(('groups', 'ctx')), parts along dimension 0, may hold values from 0 to 511, as said below
- counts: int32 [128], P(('groups', 'ctx')), parts along dimension 0, may hold values from 8 to 32
Outputs:
- attn_out: bfloat16 [128, 7168], P(('groups', 'ctx')), parts along dimension 0
There are 2 independent parts, one for each index of `groups`. A program takes and returns all parts, laid end to end along the dimension named above; an argument that names none is the same for every part. Nothing has to cross between parts.
Inputs may be any that keep to these rules, and one draw needn't show every extreme that they name: `selected`: each row lists 32 different block numbers. Over the rows 4 i to 4 i + 4 - 1 (the query tokens of one device) and their first counts entries, at most 8 different listed blocks lie in the range 32 j to 32 j + 31 for any j.
All inputs are finite; a program needn't handle non-finite values.
Results may differ from a plain program's by a relative error of at most 0.01.
The roundings to bfloat16 on the way count: a program that leaves them out, or rounds other values in their place, can miss the bound.
Values may be sent and summed in bfloat16 or wider, within the bound.
A program may use at most 128 MiB of HBM per device.

v0:
```python
import functools
import math

import jax
import jax.numpy as jnp
from jax import lax
from jax.experimental import pallas as pl
from jax.experimental.pallas import tpu as pltpu
from jax.sharding import PartitionSpec as P

BLK = 64
STEP = 8
SIDE = 2
TILES = 7
LAG = 2
PIECES = 2
SPLIT = 1

norm_eps = 1e-06
rope_base = 10000.0
EMPTY = -1e30


def rotate_rotary(rotary, positions):
    half_width = rotary.shape[-1] // 2
    freq_index = jnp.arange(half_width, dtype=jnp.float32)
    inverse_freq = jnp.exp(freq_index * (-2.0 * math.log(rope_base) / rotary.shape[-1]))
    angles = positions[:, None] * inverse_freq[None, :]
    cosine = jnp.cos(angles)[:, None, :]
    sine = jnp.sin(angles)[:, None, :]
    first_half = rotary[:, :, :half_width]
    second_half = rotary[:, :, half_width:]
    return jnp.concatenate(
        [first_half * cosine - second_half * sine, first_half * sine + second_half * cosine], axis=2
    )


def xor_permute(value, n_devices, distance):
    return lax.ppermute(value, "ctx", [(i, i ^ distance) for i in range(n_devices)])


def gather_kernel(n_devices, own_ref, out_ref, send_sems, recv_sems):
    me = lax.axis_index("ctx")
    barrier = pltpu.get_barrier_semaphore()
    for d in range(1, n_devices):
        pl.semaphore_signal(barrier, inc=1, device_id={"ctx": (me + d) % n_devices})
    pl.semaphore_wait(barrier, n_devices - 1)
    copies = [
        pltpu.make_async_remote_copy(
            src_ref=own_ref,
            dst_ref=out_ref.at[me],
            send_sem=send_sems.at[d],
            recv_sem=recv_sems.at[d],
            device_id={"ctx": (me + d) % n_devices},
        )
        for d in range(1, n_devices)
    ]
    for copy in copies:
        copy.start()
    out_ref[me] = own_ref[...]
    for copy in copies:
        copy.wait()


def gather_rows(own, n_devices):
    vmem = pl.BlockSpec(memory_space=pltpu.VMEM)
    out = pl.pallas_call(
        functools.partial(gather_kernel, n_devices),
        out_shape=jax.ShapeDtypeStruct((n_devices,) + own.shape, own.dtype),
        in_specs=[vmem],
        out_specs=vmem,
        scratch_shapes=[pltpu.SemaphoreType.DMA((n_devices,)), pltpu.SemaphoreType.DMA((n_devices,))],
        compiler_params=pltpu.CompilerParams(collective_id=0, has_side_effects=True),
        name="gather_rows",
    )(own)
    return out.reshape(n_devices * own.shape[0], own.shape[1])


def attend_kernel(
    n_parts, n_chunks, first, width_latent, heads, scale, steps_ref, list_ref, *refs
):
    cache_in = refs[:n_parts]
    q_refs = refs[n_parts : n_parts + n_chunks]
    o_refs = refs[n_parts + n_chunks : n_parts + 2 * n_chunks]
    lse_ref, keys, acc, sems = refs[n_parts + 2 * n_chunks :]
    part_blocks = cache_in[0].shape[0]
    copies = [
        pltpu.make_async_copy(
            cache_in[i], keys.at[pl.ds(i * part_blocks, part_blocks)], sems.at[i]
        )
        for i in range(n_parts)
    ]
    for copy in copies:
        copy.start()
    groups, rows_chunk, _ = o_refs[0].shape
    rows = rows_chunk * n_chunks
    tokens = rows_chunk // heads
    span = STEP * BLK
    token_of_row = (lax.broadcasted_iota(jnp.int32, (rows, 1), 0) // heads) % tokens
    row_bit = lax.shift_left(jnp.ones_like(token_of_row), token_of_row)
    block_of_col = lax.broadcasted_iota(jnp.int32, (1, span), 1) // BLK
    diagonal = lax.broadcasted_iota(jnp.int32, (rows, rows), 0) == lax.broadcasted_iota(
        jnp.int32, (rows, rows), 1
    )
    for copy in copies:
        copy.wait()
    base = 2**tokens

    def one_step(i, g, query, s, peak, total):
        entries = [list_ref[g, s * STEP + k] for k in range(STEP)]
        key_rows = jnp.concatenate([keys[e // base] for e in entries], axis=0)
        bits = jnp.zeros((1, span), jnp.int32)
        for k in range(STEP):
            bits = jnp.where(block_of_col == k, entries[k] % base, bits)
        live = (bits & row_bit) != 0
        scores = (
            lax.dot_general(
                query, key_rows, (((1,), (1,)), ((), ())), preferred_element_type=jnp.float32
            )
            * scale
        )
        scores = jnp.where(live, scores, EMPTY)
        new_peak = jnp.maximum(peak, jnp.max(scores, axis=1, keepdims=True))
        fade = jnp.exp(peak - new_peak)
        exponent = jnp.where(live, jnp.exp(scores - new_peak), 0.0)
        acc[i] = acc[i] * fade + jnp.dot(
            exponent.astype(jnp.bfloat16),
            key_rows[:, :width_latent],
            preferred_element_type=jnp.float32,
        )
        return new_peak, total * fade + jnp.sum(exponent, axis=1, keepdims=True)

    def some_groups(block, carry):
        local_g = [block * SIDE + i for i in range(SIDE)]
        g = [first + x for x in local_g]
        query = [jnp.concatenate([q[x] for q in q_refs], axis=0) for x in g]
        acc[...] = jnp.zeros_like(acc)

        def step(s, states):
            return tuple(
                one_step(i, g[i], query[i], s, *states[i]) for i in range(SIDE)
            )

        start = (jnp.full((rows, 1), EMPTY, jnp.float32), jnp.zeros((rows, 1), jnp.float32))
        n_steps = functools.reduce(jnp.maximum, [steps_ref[x] for x in g])
        states = lax.fori_loop(0, n_steps, step, (start,) * SIDE)
        for i in range(SIDE):
            peak, total = states[i]
            some = total > 0.0
            safe = jnp.where(some, total, 1.0)
            out = (acc[i] / safe).astype(jnp.bfloat16)
            for j in range(n_chunks):
                o_refs[j][local_g[i]] = out[j * rows_chunk : (j + 1) * rows_chunk]
            lse = jnp.where(some, peak + jnp.log(safe), EMPTY)
            lse_ref[pl.ds(local_g[i], 1), :] = jnp.sum(
                jnp.where(diagonal, lse, 0.0), axis=0, keepdims=True
            )
        return carry

    lax.fori_loop(0, groups // SIDE, some_groups, 0)


def attend(parts, chunks, block_list, steps, first, groups, heads, width_latent, scale):
    n_parts, n_chunks = len(parts), len(chunks)
    part_blocks, _, width_row = parts[0].shape
    rows_chunk = chunks[0].shape[1]
    vmem = pl.BlockSpec(memory_space=pltpu.VMEM)
    smem = pl.BlockSpec(memory_space=pltpu.SMEM)
    out = pl.pallas_call(
        functools.partial(attend_kernel, n_parts, n_chunks, first, width_latent, heads, scale),
        out_shape=[jax.ShapeDtypeStruct((groups, rows_chunk, width_latent), jnp.bfloat16)] * n_chunks
        + [jax.ShapeDtypeStruct((groups, rows_chunk * n_chunks), jnp.float32)],
        in_specs=[smem, smem] + [pl.BlockSpec(memory_space=pl.ANY)] * n_parts + [vmem] * n_chunks,
        out_specs=[vmem] * (n_chunks + 1),
        scratch_shapes=[
            pltpu.VMEM((n_parts * part_blocks, BLK, width_row), jnp.bfloat16),
            pltpu.VMEM((SIDE, rows_chunk * n_chunks, width_latent), jnp.float32),
            pltpu.SemaphoreType.DMA((n_parts,)),
        ],
        compiler_params=pltpu.CompilerParams(vmem_limit_bytes=48 * 2**20),
        name="attend",
        cost_estimate=pl.CostEstimate(
            flops=2 * groups * rows_chunk * n_chunks * part_blocks * BLK * (width_row + width_latent),
            bytes_accessed=2 * n_parts * part_blocks * BLK * width_row,
            transcendentals=0,
        ),
    )(steps, block_list, *parts, *chunks)
    return out[:n_chunks], out[n_chunks]


def combine(partials):
    if len(partials) == 1:
        return partials[0]
    logs = [log for _, log in partials]
    top = functools.reduce(jnp.maximum, logs)
    shares = [jnp.exp(x - top) for x in logs]
    total = functools.reduce(jnp.add, shares)
    value = functools.reduce(
        jnp.add,
        [v.astype(jnp.float32) * (s / total)[:, :, None] for (v, _), s in zip(partials, shares)],
    ).astype(jnp.bfloat16)
    return value, top + jnp.log(total)


def project_kernel(bits, tiles, rows_ref, w_ref, out_ref, weights, w_sems, *bufs):
    n_stages = len(bits)
    sends, recvs = bufs[:n_stages], bufs[n_stages : 2 * n_stages]
    send_sems, recv_sems = bufs[2 * n_stages :]
    me = lax.axis_index("ctx")
    upper = [(me // bit) % 2 for bit in bits]
    partner = [me + bit * (1 - 2 * up) for bit, up in zip(bits, upper)]
    width = weights.shape[2]
    loads = [
        pltpu.make_async_copy(
            w_ref.at[:, pl.ds(t * width, width)], weights.at[t], w_sems.at[t]
        )
        for t in range(tiles)
    ]
    for load in loads:
        load.start()
    barrier = pltpu.get_barrier_semaphore()
    for other in partner:
        pl.semaphore_signal(barrier, inc=1, device_id={"ctx": other})
    pl.semaphore_wait(barrier, n_stages)

    def copy_of(k, t):
        return pltpu.make_async_remote_copy(
            src_ref=sends[k].at[t],
            dst_ref=recvs[k].at[t],
            send_sem=send_sems.at[t, k],
            recv_sem=recv_sems.at[t, k],
            device_id={"ctx": partner[k]},
        )

    def send_half(k, t, total):
        half = total.shape[0] // 2
        low, high = total[:half], total[half:]
        sends[k][t] = jnp.where(upper[k] == 1, low, high).astype(jnp.bfloat16)
        copy_of(k, t).start()
        return jnp.where(upper[k] == 1, high, low)

    kept = {}
    for time in range(tiles + LAG * n_stages):
        for k in reversed(range(n_stages)):
            t = time - LAG * (k + 1)
            if 0 <= t < tiles:
                copy_of(k, t).wait()
                total = kept.pop(t) + recvs[k][t].astype(jnp.float32)
                if k + 1 < n_stages:
                    kept[t] = send_half(k + 1, t, total)
                else:
                    out_ref[:, t * width : (t + 1) * width] = total.astype(jnp.bfloat16)
        if time < tiles:
            loads[time].wait()
            total = jnp.dot(rows_ref[...], weights[time], preferred_element_type=jnp.float32)
            kept[time] = send_half(0, time, total)


def project(rows, weight, q_local, n_devices):
    bits = [1 << i for i in range(n_devices.bit_length() - 1)]
    depth, columns = weight.shape
    tiles = max(t for t in range(1, TILES + 1) if columns % (t * 128) == 0)
    width = columns // tiles
    sizes = [rows.shape[0] >> (i + 1) for i in range(len(bits))]
    slots = [pltpu.VMEM((tiles, size, width), jnp.bfloat16) for size in sizes]
    vmem = pl.BlockSpec(memory_space=pltpu.VMEM)
    return pl.pallas_call(
        functools.partial(project_kernel, bits, tiles),
        out_shape=jax.ShapeDtypeStruct((q_local, columns), jnp.bfloat16),
        in_specs=[vmem, pl.BlockSpec(memory_space=pl.ANY)],
        out_specs=vmem,
        scratch_shapes=[
            pltpu.VMEM((tiles, depth, width), jnp.bfloat16),
            pltpu.SemaphoreType.DMA((tiles,)),
            *slots,
            *slots,
            pltpu.SemaphoreType.DMA((tiles, len(bits))),
            pltpu.SemaphoreType.DMA((tiles, len(bits))),
        ],
        compiler_params=pltpu.CompilerParams(
            collective_id=1, has_side_effects=True, vmem_limit_bytes=48 * 2**20
        ),
        name="project",
    )(rows, weight)


def local(
    cache_bits, query_bits, q_latent, q_gain, w_uq, w_uk, w_uv, w_o, latent_cache, kv_scales, selected, counts
):
    n_devices = lax.axis_size("ctx")
    me = lax.axis_index("ctx")
    heads_local, width_content, width_latent = w_uk.shape
    width_row = latent_cache.shape[1]
    width_rotary = width_row - width_latent
    q_local, top_blocks = selected.shape
    blocks_local = latent_cache.shape[0] // BLK
    tiles = kv_scales.shape[1]

    cache_t = latent_cache.T
    scaled_t = (
        cache_t[:width_latent].astype(jnp.float32).reshape(tiles, width_latent // tiles, -1)
        * kv_scales.T[:, None, :]
    ).astype(jnp.bfloat16)
    whole_t = jnp.concatenate([scaled_t.reshape(width_latent, -1), cache_t[width_latent:]], axis=0)
    piece_blocks = blocks_local // PIECES
    own_cache = [
        x.T.reshape(piece_blocks, BLK, width_row) for x in jnp.split(whole_t, PIECES, axis=1)
    ]

    latent_f = q_latent.astype(jnp.float32)
    normed = (
        latent_f
        * lax.rsqrt(jnp.mean(latent_f * latent_f, axis=1, keepdims=True) + norm_eps)
        * q_gain
    ).astype(jnp.bfloat16)
    live_sel = jnp.arange(top_blocks, dtype=jnp.int32)[None, :] < counts[:, None]
    owner = jnp.where(live_sel, selected // blocks_local, -1)
    row_width = normed.shape[1] + 2 * top_blocks
    packed = jnp.concatenate(
        [
            normed,
            owner.astype(jnp.bfloat16),
            (selected % blocks_local).astype(jnp.bfloat16),
            jnp.zeros((q_local, -row_width % 128), jnp.bfloat16),
        ],
        axis=1,
    )
    gathered = gather_rows(packed, n_devices)
    gathered, own_cache = lax.optimization_barrier((gathered, own_cache))
    near_bit, far_bit = cache_bits
    far = [xor_permute(x, n_devices, far_bit) for x in own_cache]
    near = [xor_permute(x, n_devices, near_bit) for x in own_cache]
    parts_masks = [0, far_bit, near_bit, far_bit | near_bit]
    row_count = gathered.shape[0]
    latent_width = normed.shape[1]
    all_normed = gathered[:, :latent_width]
    all_owner = gathered[:, latent_width : latent_width + top_blocks].astype(jnp.int32)
    all_inner = gathered[:, latent_width + top_blocks : row_width].astype(jnp.int32)

    projected = jnp.dot(all_normed, w_uq, preferred_element_type=jnp.float32).reshape(
        row_count, heads_local, width_content + width_rotary
    )
    content = projected[:, :, :width_content].astype(jnp.bfloat16)
    positions = jnp.arange(row_count, dtype=jnp.int32).astype(jnp.float32)
    rotated = rotate_rotary(projected[:, :, width_content:], positions).astype(jnp.bfloat16)
    absorbed = jnp.einsum("khn,hnc->khc", content, w_uk, preferred_element_type=jnp.float32).astype(
        jnp.bfloat16
    )
    groups = row_count // q_local
    own_queries = jnp.concatenate([absorbed, rotated], axis=2).reshape(
        groups, q_local * heads_local, width_row
    )
    chunks = [own_queries]
    chunk_masks = [0]
    for bit in reversed(query_bits):
        chunks = chunks + [xor_permute(c, n_devices, bit) for c in chunks]
        chunk_masks = chunk_masks + [m | bit for m in chunk_masks]

    passed = []
    for i, piece in enumerate(far):
        j = len(chunks) - 1 if i + 1 == len(far) else 1
        far[i], chunks[j] = lax.optimization_barrier((piece, chunks[j]))
        passed.append(xor_permute(far[i], n_devices, near_bit))
    parts = own_cache + far + near + passed

    n_held = len(parts) * piece_blocks
    place = jnp.full_like(all_owner, -1)
    for i, mask in enumerate(parts_masks):
        place = jnp.where(all_owner == (me ^ mask), i * blocks_local + all_inner, place)
    held = jnp.arange(n_held, dtype=jnp.int32)
    member = jnp.any(
        place.reshape(groups, q_local, top_blocks)[:, :, :, None] == held[None, None, None, :], axis=2
    ).astype(jnp.int32)
    bits = jnp.sum(
        member * lax.shift_left(1, jnp.arange(q_local, dtype=jnp.int32))[None, :, None], axis=1
    )
    needed = (bits > 0).astype(jnp.int32)
    rank = jnp.cumsum(needed, axis=1) - needed
    entry = held[None, :] * 2**q_local + bits
    slot = (rank[:, :, None] == held[None, None, :]) & (needed[:, :, None] == 1)
    block_list = jnp.sum(jnp.where(slot, entry[:, :, None], 0), axis=1)
    steps = (jnp.sum(needed, axis=1) + STEP - 1) // STEP

    scale = 1.0 / math.sqrt(width_content + width_rotary)
    rows_chunk = q_local * heads_local
    groups_call = groups // SPLIT
    halves = []
    for first in range(0, groups, groups_call):
        outs, lse = attend(
            parts, chunks, block_list, steps, first, groups_call, heads_local, width_latent, scale
        )
        held_for = {
            mask: [(outs[i], lse[:, i * rows_chunk : (i + 1) * rows_chunk])]
            for i, mask in enumerate(chunk_masks)
        }
        for bit in query_bits:
            leaving = sorted([m for m in held_for if m & bit], reverse=True)
            going = [combine(held_for.pop(m)) for m in leaving]
            logs = xor_permute(jnp.stack([log for _, log in going]), n_devices, bit)
            for i, mask in enumerate(leaving):
                value = xor_permute(going[i][0], n_devices, bit)
                held_for[mask ^ bit].append((value, logs[i]))
        halves.append(combine(held_for[0])[0])
    latent_out = jnp.concatenate(halves, axis=0)
    head_out = latent_out.reshape(row_count, heads_local, width_latent)
    head_values = jnp.einsum(
        "qhc,hcv->qhv", head_out, w_uv, preferred_element_type=jnp.float32
    ).astype(jnp.bfloat16)
    n_bits = n_devices.bit_length() - 1
    rows = head_values.reshape((2,) * n_bits + (q_local, -1))
    rows = rows.transpose(tuple(reversed(range(n_bits))) + (n_bits, n_bits + 1))
    return project(rows.reshape(row_count, -1), w_o, q_local, n_devices)


def solution(mesh):
    n_devices = mesh.shape["ctx"]
    all_bits = [1 << i for i in range(n_devices.bit_length() - 1)]
    cache_bits, query_bits = all_bits[:2], all_bits[2:]
    in_specs = (
        P(("groups", "ctx"), None),
        P(),
        P(None, "ctx"),
        P("ctx", None, None),
        P("ctx", None, None),
        P("ctx", None),
        P(("groups", "ctx"), None),
        P(("groups", "ctx"), None),
        P(("groups", "ctx"), None),
        P(("groups", "ctx")),
    )
    out_specs = P(("groups", "ctx"), None)
    return jax.shard_map(
        functools.partial(local, cache_bits, query_bits),
        mesh=mesh,
        in_specs=in_specs,
        out_specs=out_specs,
        check_vma=False,
    )
```

profile of v0, /device:TPU:0, one launch (start us, length us, event | category | flops | bytes accessed | tf_op | source)
XLA Modules:
  0.0 191.8 jit_solution(17869819840216871504)
XLA Ops:
  0.0 0.9 fusion.14
  0.9 0.8 fusion.24
  1.7 0.8 fusion.16
  2.5 0.7 concatenate.12.own_ref
  3.2 11.7 %gather_rows.1 = bf16[16,4,1664]{2,1,0:T(4,128)(2,1)} custom-call(bf16[4,1664]{1,0:T(4,128)(2,1)} %concatenate.12.own_ref), custom_call_target="tpu_custom_call" | custom-call | tf_op jit(solution)/shard_map/gather_rows/pallas_call | solution.py:67
  14.9 1.7 reshape.142
  16.6 1.0 slice.61
  17.5 2.1 %fusion = bf16[512,2048]{1,0:T(8,128)(2,1)S(1)} fusion(bf16[576,2048]{1,0:T(8,128)(2,1)} %bitcast.97, f32[4,2048]{1,0:T(4,128)} %bitcast.101), kind=kLoop, calls=%fused_computation.1 | loop fusion | flops 3145728 | bytes 4227072 | tf_op jit(solution)/shard_map/convert_element_type | solution.py:303
  19.6 0.2 fusion.4
  19.9 1.4 copy.28
  21.3 0.7 copy.27
  22.0 2.3 %collective-permute-start = (bf16[16,64,576]{2,1,0:T(8,128)(2,1)S(1)}, bf16[16,64,576]{2,1,0:T(8,128)(2,1)}, u32[]{:S(2)}, u32[]{:S(2)}) collective-permute-start(bf16[16,64,576]{2,1,0:T(8,128)(2,1)S(1)} %bitcast.90), channel_id=1, source_target_pairs={{0,2},{1,3},{2,0},{3,1},{4,6},{5,7},{6,4},{7,5},{8,10},{9,11},{10,... | collective-permute-start | bytes 3538952 | tf_op jit(solution)/shard_map/ppermute | solution.py:39
  24.3 3.4 %fusion.9 = f32[64,1536]{1,0:T(8,128)S(1)} fusion(bf16[1536,1536]{1,0:T(8,128)(2,1)} %param.12, bf16[64,1664]{1,0:T(8,128)(2,1)} %reshape.142), kind=kOutput, calls=%fused_computation.24 | convolution fusion | flops 301989888 | bytes 5308416 | tf_op jit(solution)/shard_map/dot_general | solution.py:340
  27.7 0.2 reshape.145
  27.9 0.1 fusion.26
  28.0 0.2 multiply_cosine_fusion
  28.2 0.3 fusion.1
  28.5 0.1 subtract_convert_fusion
  28.7 0.1 pad_maximum_fusion.1
  28.8 0.4 copy.33
  29.2 1.9 collective-permute-start.1
  31.1 29.7 %collective-permute-done.1.refs_9_ = bf16[16,32,576]{2,1,0:T(8,128)(2,1)} collective-permute-done((bf16[16,32,576]{2,1,0:T(8,128)(2,1)S(1)}, bf16[16,32,576]{2,1,0:T(8,128)(2,1)}, u32[]{:S(2)}, u32[]{:S(2)}) %collective-permute-start.1) | collective-permute-done | bytes 589856 | tf_op jit(solution)/shard_map/ppermute | solution.py:39
  60.8 2.0 %collective-permute-start.8 = (bf16[16,32,576]{2,1,0:T(8,128)(2,1)S(1)}, bf16[16,32,576]{2,1,0:T(8,128)(2,1)}, u32[]{:S(2)}, u32[]{:S(2)}) collective-permute-start(bf16[16,32,576]{2,1,0:T(8,128)(2,1)S(1)} %bitcast.94), channel_id=1, source_target_pairs={{0,4},{1,5},{2,6},{3,7},{4,0},{5,1},{6,2},{7,3},{8,12},{9,13},{10,... | collective-permute-start | bytes 1769480 | tf_op jit(solution)/shard_map/ppermute | solution.py:39
  62.8 0.9 fusion.11
  63.7 0.4 fusion.6
  64.1 0.6 collective-permute-start.5
  64.6 14.0 %collective-permute-done.3.refs_11_ = bf16[16,32,576]{2,1,0:T(8,128)(2,1)} collective-permute-done((bf16[16,32,576]{2,1,0:T(8,128)(2,1)}, bf16[16,32,576]{2,1,0:T(8,128)(2,1)}, u32[]{:S(2)}, u32[]{:S(2)}) %collective-permute-start.3) | collective-permute-done | bytes 589856 | tf_op jit(solution)/shard_map/ppermute | solution.py:39
  78.7 2.9 %collective-permute-done.2.refs_3_ = bf16[16,64,576]{2,1,0:T(8,128)(2,1)} collective-permute-done((bf16[16,64,576]{2,1,0:T(8,128)(2,1)}, bf16[16,64,576]{2,1,0:T(8,128)(2,1)}, u32[]{:S(2)}, u32[]{:S(2)}) %collective-permute-start.2) | collective-permute-done | bytes 1179680 | tf_op jit(solution)/shard_map/ppermute | solution.py:39
  81.6 0.1 select_reduce_fusion.1
  81.7 0.3 reduce_window_sum.11
  82.0 0.1 convert_subtract_fusion
  82.1 1.2 select_reduce_fusion.list_ref
  83.3 7.5 %collective-permute-done.8.refs_10_ = bf16[16,32,576]{2,1,0:T(8,128)(2,1)} collective-permute-done((bf16[16,32,576]{2,1,0:T(8,128)(2,1)S(1)}, bf16[16,32,576]{2,1,0:T(8,128)(2,1)}, u32[]{:S(2)}, u32[]{:S(2)}) %collective-permute-start.8) | collective-permute-done | bytes 589856 | tf_op jit(solution)/shard_map/ppermute | solution.py:39
  90.8 26.0 %attend.1 = (bf16[16,32,512]{2,1,0:T(8,128)(2,1)S(1)}, bf16[16,32,512]{2,1,0:T(8,128)(2,1)S(1)}, bf16[16,32,512]{2,1,0:T(8,128)(2,1)S(1)}, bf16[16,32,512]{2,1,0:T(8,128)(2,1)S(1)}, f32[16,128]{1,0:T(8,128)S(1)}) custom-call(s32[16]{0:T(128)S(1)} %and_select_fusion.steps_ref, s32[16,128]{1,0:T(8,128)S(1)} %select_reduce_fusion.list_ref, ...), custom_call_target="tpu_custom_call" | custom-call | flops 4563402752 | bytes 9437184 | tf_op jit(solution)/shard_map/attend/pallas_call | solution.py:169
  116.9 2.0 %collective-permute-start.9 = (f32[2,16,32]{2,1,0:T(8,128)S(1)}, f32[2,16,32]{2,1,0:T(8,128)S(1)}, u32[]{:S(2)}, u32[]{:S(2)}) collective-permute-start(f32[2,16,32]{2,1,0:T(8,128)S(1)} %pad_maximum_fusion.2), channel_id=1, source_target_pairs={{0,4},{1,5},{2,6},{3,7},{4,0},{5,1},{6,2},{7,3},{8,12},{9,13},{10,... | collective-permute-start | bytes 12296 | tf_op jit(solution)/shard_map/ppermute | solution.py:39
  118.9 10.3 %collective-permute-done.9 = f32[2,16,32]{2,1,0:T(8,128)S(1)} collective-permute-done((f32[2,16,32]{2,1,0:T(8,128)S(1)}, f32[2,16,32]{2,1,0:T(8,128)S(1)}, u32[]{:S(2)}, u32[]{:S(2)}) %collective-permute-start.9) | collective-permute-done | bytes 4128 | tf_op jit(solution)/shard_map/ppermute | solution.py:39
  129.2 0.1 add_bitcast_fusion
  129.2 11.6 %collective-permute-start.10 = (f32[1,16,32]{2,1,0:T(8,128)S(1)}, f32[1,16,32]{2,1,0:T(8,128)S(1)}, u32[]{:S(2)}, u32[]{:S(2)}) collective-permute-start(f32[1,16,32]{2,1,0:T(8,128)S(1)} %add_bitcast_fusion), channel_id=1, source_target_pairs={{0,8},{1,9},{2,10},{3,11},{4,12},{5,13},{6,14},{7,15},{8,0},{9,1},... | collective-permute-start | bytes 6152 | tf_op jit(solution)/shard_map/ppermute | solution.py:39
  140.9 1.7 collective-permute-start.11
  142.7 0.3 add_convert_fusion.1
  143.0 3.0 %collective-permute-start.13 = (bf16[16,32,512]{2,1,0:T(8,128)(2,1)S(1)}, bf16[16,32,512]{2,1,0:T(8,128)(2,1)S(1)}, u32[]{:S(2)}, u32[]{:S(2)}) collective-permute-start(bf16[16,32,512]{2,1,0:T(8,128)(2,1)S(1)} %add_convert_fusion.1), channel_id=1, source_target_pairs={{0,8},{1,9},{2,10},{3,11},{4,12},{5,13},{6,14},{7,15},{8,0},{9,1},... | collective-permute-start | bytes 1572872 | tf_op jit(solution)/shard_map/ppermute | solution.py:39
  146.0 15.7 %collective-permute-done.11 = bf16[16,32,512]{2,1,0:T(8,128)(2,1)S(1)} collective-permute-done((bf16[16,32,512]{2,1,0:T(8,128)(2,1)S(1)}, bf16[16,32,512]{2,1,0:T(8,128)(2,1)S(1)}, u32[]{:S(2)}, u32[]{:S(2)}) %collective-permute-start.11) | collective-permute-done | bytes 524320 | tf_op jit(solution)/shard_map/ppermute | solution.py:39
  161.7 5.1 %collective-permute-done.13 = bf16[16,32,512]{2,1,0:T(8,128)(2,1)S(1)} collective-permute-done((bf16[16,32,512]{2,1,0:T(8,128)(2,1)S(1)}, bf16[16,32,512]{2,1,0:T(8,128)(2,1)S(1)}, u32[]{:S(2)}, u32[]{:S(2)}) %collective-permute-start.13) | collective-permute-done | bytes 524320 | tf_op jit(solution)/shard_map/ppermute | solution.py:39
  166.8 0.4 add_convert_fusion
  167.2 0.4 fusion.5
  167.6 0.1 copy.35
  167.9 23.3 %project.1 = bf16[4,7168]{1,0:T(4,128)(2,1)S(1)} custom-call(bf16[64,1024]{1,0:T(8,128)(2,1)S(1)} %reshape.149.rows_ref, bf16[1024,7168]{1,0:T(8,128)(2,1)} %w_ref.1), custom_call_target="tpu_custom_call" | custom-call | tf_op jit(solution)/shard_map/project/pallas_call | solution.py:267
  191.2 0.6 copy.50
  (34 shorter events, 0.4 us)
Async XLA Ops:
  0.0 28.2 %copy-start = (bf16[8,128,512]{2,1,0:T(8,128)(2,1)S(1)}, bf16[8,128,512]{2,1,0:T(8,128)(2,1)}, u32[]{:S(2)}) copy-start(bf16[8,128,512]{2,1,0:T(8,128)(2,1)} %param.13) | copy-start | bytes 3145732
  22.0 42.0 %collective-permute-start = (bf16[16,64,576]{2,1,0:T(8,128)(2,1)S(1)}, bf16[16,64,576]{2,1,0:T(8,128)(2,1)}, u32[]{:S(2)}, u32[]{:S(2)}) collective-permute-start(bf16[16,64,576]{2,1,0:T(8,128)(2,1)S(1)} %bitcast.90), channel_id=1, source_target_pairs={{0,2},{1,3},{2,0},{3,1},{4,6},{5,7},{6,4},{7,5},{8,10},{9,11},{10,... | collective-permute-start | bytes 3538952 | tf_op jit(solution)/shard_map/ppermute | solution.py:39
  29.2 31.6 %collective-permute-start.1 = (bf16[16,32,576]{2,1,0:T(8,128)(2,1)S(1)}, bf16[16,32,576]{2,1,0:T(8,128)(2,1)}, u32[]{:S(2)}, u32[]{:S(2)}) collective-permute-start(bf16[16,32,576]{2,1,0:T(8,128)(2,1)S(1)} %bitcast.93), channel_id=1, source_target_pairs={{0,8},{1,9},{2,10},{3,11},{4,12},{5,13},{6,14},{7,15},{8,0},{9,1},... | collective-permute-start | bytes 1769480 | tf_op jit(solution)/shard_map/ppermute | solution.py:39
  31.1 50.5 %collective-permute-start.2 = (bf16[16,64,576]{2,1,0:T(8,128)(2,1)}, bf16[16,64,576]{2,1,0:T(8,128)(2,1)}, u32[]{:S(2)}, u32[]{:S(2)}) collective-permute-start(bf16[16,64,576]{2,1,0:T(8,128)(2,1)} %bitcast.6.refs_1_), channel_id=1, source_target_pairs={{0,2},{1,3},{2,0},{3,1},{4,6},{5,7},{6,4},{7,5},{8,10},{9,11},{10,... | collective-permute-start | bytes 3538952 | tf_op jit(solution)/shard_map/ppermute | solution.py:39
  60.8 17.9 %collective-permute-start.3 = (bf16[16,32,576]{2,1,0:T(8,128)(2,1)}, bf16[16,32,576]{2,1,0:T(8,128)(2,1)}, u32[]{:S(2)}, u32[]{:S(2)}) collective-permute-start(bf16[16,32,576]{2,1,0:T(8,128)(2,1)} %collective-permute-done.1.refs_9_), channel_id=1, source_target_pairs={{0,4},{1,5},{2,6},{3,7},{4,0},{5,1},{6,2},{7,3},{8,12},{9,13},{10,... | collective-permute-start | bytes 1769480 | tf_op jit(solution)/shard_map/ppermute | solution.py:39
  60.8 30.0 %collective-permute-start.8 = (bf16[16,32,576]{2,1,0:T(8,128)(2,1)S(1)}, bf16[16,32,576]{2,1,0:T(8,128)(2,1)}, u32[]{:S(2)}, u32[]{:S(2)}) collective-permute-start(bf16[16,32,576]{2,1,0:T(8,128)(2,1)S(1)} %bitcast.94), channel_id=1, source_target_pairs={{0,4},{1,5},{2,6},{3,7},{4,0},{5,1},{6,2},{7,3},{8,12},{9,13},{10,... | collective-permute-start | bytes 1769480 | tf_op jit(solution)/shard_map/ppermute | solution.py:39
  62.8 28.0 %collective-permute-start.4 = (bf16[16,64,576]{2,1,0:T(8,128)(2,1)S(1)}, bf16[16,64,576]{2,1,0:T(8,128)(2,1)}, u32[]{:S(2)}, u32[]{:S(2)}) collective-permute-start(bf16[16,64,576]{2,1,0:T(8,128)(2,1)S(1)} %bitcast.91), channel_id=1, source_target_pairs={{0,1},{1,0},{2,3},{3,2},{4,5},{5,4},{6,7},{7,6},{8,9},{9,8},{10,11... | collective-permute-start | bytes 3538952 | tf_op jit(solution)/shard_map/ppermute | solution.py:39
  64.1 26.7 %collective-permute-start.5 = (bf16[16,64,576]{2,1,0:T(8,128)(2,1)}, bf16[16,64,576]{2,1,0:T(8,128)(2,1)}, u32[]{:S(2)}, u32[]{:S(2)}) collective-permute-start(bf16[16,64,576]{2,1,0:T(8,128)(2,1)} %bitcast.6.refs_1_), channel_id=1, source_target_pairs={{0,1},{1,0},{2,3},{3,2},{4,5},{5,4},{6,7},{7,6},{8,9},{9,8},{10,11... | collective-permute-start | bytes 3538952 | tf_op jit(solution)/shard_map/ppermute | solution.py:39
  78.7 12.1 %collective-permute-start.6 = (bf16[16,64,576]{2,1,0:T(8,128)(2,1)}, bf16[16,64,576]{2,1,0:T(8,128)(2,1)}, u32[]{:S(2)}, u32[]{:S(2)}) collective-permute-start(bf16[16,64,576]{2,1,0:T(8,128)(2,1)} %collective-permute-done.refs_2_), channel_id=1, source_target_pairs={{0,1},{1,0},{2,3},{3,2},{4,5},{5,4},{6,7},{7,6},{8,9},{9,8},{10,11... | collective-permute-start | bytes 3538952 | tf_op jit(solution)/shard_map/ppermute | solution.py:39
  81.6 9.2 %collective-permute-start.7 = (bf16[16,64,576]{2,1,0:T(8,128)(2,1)}, bf16[16,64,576]{2,1,0:T(8,128)(2,1)}, u32[]{:S(2)}, u32[]{:S(2)}) collective-permute-start(bf16[16,64,576]{2,1,0:T(8,128)(2,1)} %collective-permute-done.2.refs_3_), channel_id=1, source_target_pairs={{0,1},{1,0},{2,3},{3,2},{4,5},{5,4},{6,7},{7,6},{8,9},{9,8},{10,11... | collective-permute-start | bytes 3538952 | tf_op jit(solution)/shard_map/ppermute | solution.py:39
  116.8 50.5 %copy-start.1 = (bf16[8,512,128]{2,1,0:T(8,128)(2,1)S(1)}, bf16[8,512,128]{2,1,0:T(8,128)(2,1)}, u32[]{:S(2)}) copy-start(bf16[8,512,128]{2,1,0:T(8,128)(2,1)} %param.14) | copy-start | bytes 3145732
  116.8 25.9 %collective-permute-start.12 = (bf16[16,32,512]{2,1,0:T(8,128)(2,1)S(1)}, bf16[16,32,512]{2,1,0:T(8,128)(2,1)S(1)}, u32[]{:S(2)}, u32[]{:S(2)}) collective-permute-start(bf16[16,32,512]{2,1,0:T(8,128)(2,1)S(1)} %get-tuple-element.28), channel_id=1, source_target_pairs={{0,4},{1,5},{2,6},{3,7},{4,0},{5,1},{6,2},{7,3},{8,12},{9,13},{10,... | collective-permute-start | bytes 1572872 | tf_op jit(solution)/shard_map/ppermute | solution.py:39
  116.9 12.3 %collective-permute-start.9 = (f32[2,16,32]{2,1,0:T(8,128)S(1)}, f32[2,16,32]{2,1,0:T(8,128)S(1)}, u32[]{:S(2)}, u32[]{:S(2)}) collective-permute-start(f32[2,16,32]{2,1,0:T(8,128)S(1)} %pad_maximum_fusion.2), channel_id=1, source_target_pairs={{0,4},{1,5},{2,6},{3,7},{4,0},{5,1},{6,2},{7,3},{8,12},{9,13},{10,... | collective-permute-start | bytes 12296 | tf_op jit(solution)/shard_map/ppermute | solution.py:39
  129.2 13.4 %collective-permute-start.10 = (f32[1,16,32]{2,1,0:T(8,128)S(1)}, f32[1,16,32]{2,1,0:T(8,128)S(1)}, u32[]{:S(2)}, u32[]{:S(2)}) collective-permute-start(f32[1,16,32]{2,1,0:T(8,128)S(1)} %add_bitcast_fusion), channel_id=1, source_target_pairs={{0,8},{1,9},{2,10},{3,11},{4,12},{5,13},{6,14},{7,15},{8,0},{9,1},... | collective-permute-start | bytes 6152 | tf_op jit(solution)/shard_map/ppermute | solution.py:39
  140.9 20.8 %collective-permute-start.11 = (bf16[16,32,512]{2,1,0:T(8,128)(2,1)S(1)}, bf16[16,32,512]{2,1,0:T(8,128)(2,1)S(1)}, u32[]{:S(2)}, u32[]{:S(2)}) collective-permute-start(bf16[16,32,512]{2,1,0:T(8,128)(2,1)S(1)} %get-tuple-element.26), channel_id=1, source_target_pairs={{0,4},{1,5},{2,6},{3,7},{4,0},{5,1},{6,2},{7,3},{8,12},{9,13},{10,... | collective-permute-start | bytes 1572872 | tf_op jit(solution)/shard_map/ppermute | solution.py:39
  143.0 23.8 %collective-permute-start.13 = (bf16[16,32,512]{2,1,0:T(8,128)(2,1)S(1)}, bf16[16,32,512]{2,1,0:T(8,128)(2,1)S(1)}, u32[]{:S(2)}, u32[]{:S(2)}) collective-permute-start(bf16[16,32,512]{2,1,0:T(8,128)(2,1)S(1)} %add_convert_fusion.1), channel_id=1, source_target_pairs={{0,8},{1,9},{2,10},{3,11},{4,12},{5,13},{6,14},{7,15},{8,0},{9,1},... | collective-permute-start | bytes 1572872 | tf_op jit(solution)/shard_map/ppermute | solution.py:39
where the time goes:
time: 191 us; the launch traced here: 192 us
  waiting for transfers between devices  85.2 us (45%)
  Pallas kernels  61 us (32%)
  starting transfers between devices  25.2 us (13%)
  other arithmetic  9.01 us (5%)
  local copies, waits for them, and re-layouts  7.08 us (4%)
  matrix products  4.05 us (2%)
    ppermute x14, waiting for transfers between devices, xor_permute(): lax.ppermute(value, 'ctx', [(i, i ^ distance) for i in range(n_devices)])  85.2 us
    pallas_call x1, Pallas kernels, attend(): pl.pallas_call(functools.partial(attend_kernel, n_parts, n_chunks, first,...  26 us
    ppermute x14, starting transfers between devices, xor_permute(): lax.ppermute(value, 'ctx', [(i, i ^ distance) for i in range(n_devices)])  25.2 us
    pallas_call x1, Pallas kernels, project(): pl.pallas_call(functools.partial(project_kernel, bits, tiles), out_shape=...  23.3 us
    pallas_call x1, Pallas kernels, gather_rows(): pl.pallas_call(functools.partial(gather_kernel, n_devices), out_shape=jax...  11.7 us
  transfers between devices with their start and end apart: 14, of which 7 were waited for; matrix products, arithmetic and copies ran while one was open for 4% of the time, Pallas kernels for 0%

commit v1 on v0

v1 whole, which is shorter than its diff:
```python
import functools
import math

import jax
import jax.numpy as jnp
from jax import lax
from jax.experimental import pallas as pl
from jax.experimental.pallas import tpu as pltpu
from jax.sharding import PartitionSpec as P

BLK = 64
SIDE = 2
TILES = 7
LAG = 2
KEY_PIECES = 8
QUERY_PIECES = 4

norm_eps = 1e-06
rope_base = 10000.0
EMPTY = -1e30


def exchange_kernel(
    cache_bits, query_bits, q_ref, gain_ref, sel_ref, scales_ref, w_uq_ref, w_uk_ref, cache_ref,
    keys_ref, rots_ref, q_out_ref, q_rot_ref, sel_out_ref, q_in, gain, scales, raw, w_uq, w_uk,
    normed, lat, rows_x, rows_q, rows_r, q_pack, load_sems, gather_send, gather_recv, key_send,
    key_recv, q_send, q_recv,
):
    n_devices = lat.shape[0]
    me = lax.axis_index("ctx")
    near_bit, far_bit = cache_bits
    q_local, width_q = q_ref.shape
    width_row, span = raw.shape
    n_tiles = scales_ref.shape[0]
    heads, width_content, width_latent = w_uk.shape
    width_rotary = width_row - width_latent
    width_head = width_content + width_rotary
    _, blocks, blk, _ = keys_ref.shape
    n_chunks, groups, rows, _ = q_out_ref.shape
    key_step = blocks // KEY_PIECES
    q_step = groups // QUERY_PIECES
    key_span = span // KEY_PIECES
    tokens = n_devices * q_local
    half = width_rotary // 2

    def peer(bit):
        return me + bit * (1 - 2 * ((me // bit) % 2))

    def key_load(i):
        part = pl.ds(i * key_span, key_span)
        return pltpu.make_async_copy(
            cache_ref.at[:width_latent, part], raw.at[:width_latent, part], load_sems.at[i]
        )

    others = [
        pltpu.make_async_copy(source, target, load_sems.at[KEY_PIECES + k])
        for k, (source, target) in enumerate(
            (
                (q_ref, q_in),
                (gain_ref, gain),
                (scales_ref, scales),
                (cache_ref.at[width_latent:], raw.at[width_latent:]),
                (w_uq_ref, w_uq),
                (w_uk_ref, w_uk),
            )
        )
    ]
    q_load, gain_load, scales_load, rot_load, w_uq_load, w_uk_load = others
    q_load.start()
    gain_load.start()
    scales_load.start()
    rot_load.start()
    for i in range(KEY_PIECES):
        key_load(i).start()
    w_uq_load.start()
    w_uk_load.start()
    barrier = pltpu.get_barrier_semaphore()
    for d in range(1, n_devices):
        pl.semaphore_signal(barrier, inc=1, device_id={"ctx": (me + d) % n_devices})

    q_load.wait()
    gain_load.wait()
    latent = q_in[...].astype(jnp.float32)
    mean = jnp.mean(latent * latent, axis=1, keepdims=True)
    normed[...] = (latent * lax.rsqrt(mean + norm_eps) * gain[...]).astype(jnp.bfloat16)
    rot_load.wait()
    halfway = span // 2
    stacked = jnp.concatenate(
        [raw[width_latent:, :halfway], raw[width_latent:, halfway:]], axis=0
    ).astype(jnp.float32)
    rots_ref[0, : blocks // 2] = stacked.T.astype(jnp.bfloat16).reshape(blocks // 2, blk, -1)

    def key_copy(kind, i):
        source, target, bit = ((0, 1, near_bit), (0, 2, far_bit), (2, 3, near_bit))[kind]
        if i == KEY_PIECES:
            ref, piece = rots_ref, pl.ds(0, blocks // 2)
        else:
            ref, piece = keys_ref, pl.ds(i * key_step, key_step)
        return pltpu.make_async_remote_copy(
            src_ref=ref.at[source, piece],
            dst_ref=ref.at[target, piece],
            send_sem=key_send.at[kind, i],
            recv_sem=key_recv.at[kind, i],
            device_id={"ctx": peer(bit)},
        )

    def scale_piece(i):
        key_load(i).wait()
        part = slice(i * key_span, (i + 1) * key_span)
        deep = width_latent // n_tiles
        for c in range(n_tiles):
            strip = (
                raw[c * deep : (c + 1) * deep, part].astype(jnp.float32) * scales[c : c + 1, part]
            )
            keys_ref[0, i * key_step : (i + 1) * key_step, :, c * deep : (c + 1) * deep] = (
                strip.T.astype(jnp.bfloat16).reshape(key_step, blk, deep)
            )

    pl.semaphore_wait(barrier, n_devices - 1)
    gathers = []
    for d in range(1, n_devices):
        for k, (source, target) in enumerate(((normed, lat), (sel_ref, sel_out_ref))):
            gathers.append(
                pltpu.make_async_remote_copy(
                    src_ref=source,
                    dst_ref=target.at[me],
                    send_sem=gather_send.at[k, d],
                    recv_sem=gather_recv.at[k, d],
                    device_id={"ctx": (me + d) % n_devices},
                )
            )
    for copy in gathers:
        copy.start()
    key_copy(1, KEY_PIECES).start()
    key_copy(0, KEY_PIECES).start()
    lat[me] = normed[...]
    sel_out_ref[me] = sel_ref[...]
    scales_load.wait()
    for i in range(KEY_PIECES):
        scale_piece(i)
        key_copy(1, i).start()
        key_copy(0, i).start()
    lane = lax.broadcasted_iota(jnp.int32, (tokens, width_rotary), 1)
    position = lax.broadcasted_iota(jnp.int32, (tokens, width_rotary), 0).astype(jnp.float32)
    frequency = jnp.exp((lane % half).astype(jnp.float32) * (-2.0 * math.log(rope_base) / width_rotary))
    cosine = jnp.cos(position * frequency)
    sine = jnp.sin(position * frequency) * jnp.where(lane < half, -1.0, 1.0)
    w_uq_load.wait()
    w_uk_load.wait()
    for copy in gathers:
        copy.wait()
    for d in range(n_devices):
        rows_x[d * q_local : (d + 1) * q_local] = lat[d].astype(jnp.float32)
    projected = jnp.dot(
        rows_x[...].astype(jnp.bfloat16), w_uq[...], preferred_element_type=jnp.float32
    )
    for h in range(heads):
        head = projected[:, h * width_head : (h + 1) * width_head]
        rotary = head[:, width_content:]
        swapped = jnp.concatenate([rotary[:, half:], rotary[:, :half]], axis=1)
        rows_r[:, h, :] = rotary * cosine + swapped * sine
    pairs = jnp.concatenate([rows_r[: tokens // 2], rows_r[tokens // 2 :]], axis=2)
    q_pack[0] = pairs.reshape(groups // 2, rows, 2 * width_rotary).astype(jnp.bfloat16)

    stages = [(i, bit) for i, bit in enumerate(reversed(query_bits))]

    def q_copy(stage, source, j):
        target = 2**stage + source
        if j == QUERY_PIECES:
            ref, piece = q_pack, pl.ds(0, groups // 2)
        else:
            ref, piece = q_out_ref, pl.ds(j * q_step, q_step)
        return pltpu.make_async_remote_copy(
            src_ref=ref.at[source, piece],
            dst_ref=ref.at[target, piece],
            send_sem=q_send.at[target, j],
            recv_sem=q_recv.at[target, j],
            device_id={"ctx": peer(stages[stage][1])},
        )

    for h in range(heads):
        rows_q[:, h, :] = jnp.dot(
            projected[:, h * width_head : h * width_head + width_content].astype(jnp.bfloat16),
            w_uk[h],
            preferred_element_type=jnp.float32,
        )
    for j in range(QUERY_PIECES):
        first = j * q_step
        q_out_ref[0, first : first + q_step] = (
            rows_q[first * q_local : (first + q_step) * q_local]
            .reshape(q_step, rows, width_latent)
            .astype(jnp.bfloat16)
        )
        for stage, _ in stages:
            q_copy(stage, 0, j).start()
    for stage, _ in stages:
        q_copy(stage, 0, QUERY_PIECES).start()

    low_lane = lax.broadcasted_iota(jnp.int32, (groups // 2, rows, 2 * width_rotary), 2) < width_rotary

    def unpack_query(slot):
        pair = q_pack[slot].astype(jnp.float32)
        rolled = jnp.concatenate([pair[:, :, width_rotary:], pair[:, :, :width_rotary]], axis=2)
        q_rot_ref[slot, : groups // 2] = jnp.where(low_lane, pair, 0.0).astype(jnp.bfloat16)
        q_rot_ref[slot, groups // 2 :] = jnp.where(low_lane, rolled, 0.0).astype(jnp.bfloat16)

    def unpack_rots(slot):
        pair = rots_ref[slot, : blocks // 2].astype(jnp.float32)
        rolled = jnp.concatenate([pair[:, :, width_rotary:], pair[:, :, :width_rotary]], axis=2)
        rots_ref[slot, blocks // 2 :] = rolled.astype(jnp.bfloat16)

    unpack_query(0)
    unpack_rots(0)
    key_copy(0, KEY_PIECES).wait_recv()
    unpack_rots(1)
    arrivals = [(0.0, "key", KEY_PIECES, 0)]
    for i in range(KEY_PIECES):
        arrivals.append(((i + 1.0) / KEY_PIECES, "key", i, 0))
    for j in range(QUERY_PIECES + 1):
        for slot in range(1, n_chunks):
            at = 0.15 + 0.85 * (slot * QUERY_PIECES + j + 1.0) / (n_chunks * QUERY_PIECES)
            arrivals.append((at, "query", slot, j))
    for _, what, a, b in sorted(arrivals):
        if what == "key":
            key_copy(1, a).wait_recv()
            key_copy(2, a).start()
            if a == KEY_PIECES:
                unpack_rots(2)
        else:
            stage = a.bit_length() - 1
            q_copy(stage, a - 2**stage, b).wait_recv()
            for later in range(stage + 1, len(stages)):
                q_copy(later, a, b).start()
            if b == QUERY_PIECES:
                unpack_query(a)
    key_copy(2, KEY_PIECES).wait_recv()
    unpack_rots(3)
    for i in range(KEY_PIECES + 1):
        if i < KEY_PIECES:
            key_copy(0, i).wait_recv()
            key_copy(2, i).wait_recv()
        for kind in range(3):
            key_copy(kind, i).wait_send()
    for j in range(QUERY_PIECES + 1):
        for slot in range(1, n_chunks):
            stage = slot.bit_length() - 1
            q_copy(stage, slot - 2**stage, j).wait_send()


def exchange(
    cache_bits, query_bits, n_devices, q_latent, q_gain, listed, w_uq, w_uk, latent_cache, kv_scales
):
    q_local, width_q = q_latent.shape
    heads, _, width_latent = w_uk.shape
    span, width_row = latent_cache.shape
    blocks = span // BLK
    tokens = n_devices * q_local
    groups = n_devices
    n_chunks = 2 ** len(query_bits)
    rows = q_local * heads
    width_rotary = width_row - width_latent
    vmem = pl.BlockSpec(memory_space=pltpu.VMEM)
    any_space = pl.BlockSpec(memory_space=pl.ANY)
    return pl.pallas_call(
        functools.partial(exchange_kernel, cache_bits, query_bits),
        out_shape=[
            jax.ShapeDtypeStruct((4, blocks, BLK, width_latent), jnp.bfloat16),
            jax.ShapeDtypeStruct((4, blocks, BLK, 2 * width_rotary), jnp.bfloat16),
            jax.ShapeDtypeStruct((n_chunks, groups, rows, width_latent), jnp.bfloat16),
            jax.ShapeDtypeStruct((n_chunks, groups, rows, 2 * width_rotary), jnp.bfloat16),
            jax.ShapeDtypeStruct((n_devices,) + listed.shape, jnp.int32),
        ],
        in_specs=[any_space] * 2 + [vmem] + [any_space] * 4,
        out_specs=[vmem] * 5,
        scratch_shapes=[
            pltpu.VMEM(q_latent.shape, jnp.bfloat16),
            pltpu.VMEM((1, width_q), jnp.float32),
            pltpu.VMEM(kv_scales.shape[::-1], jnp.float32),
            pltpu.VMEM((width_row, span), jnp.bfloat16),
            pltpu.VMEM(w_uq.shape, jnp.bfloat16),
            pltpu.VMEM(w_uk.shape, jnp.bfloat16),
            pltpu.VMEM(q_latent.shape, jnp.bfloat16),
            pltpu.VMEM((n_devices,) + q_latent.shape, jnp.bfloat16),
            pltpu.VMEM((tokens, width_q), jnp.float32),
            pltpu.VMEM((tokens, heads, width_latent), jnp.float32),
            pltpu.VMEM((tokens, heads, width_rotary), jnp.float32),
            pltpu.VMEM((n_chunks, groups // 2, rows, 2 * width_rotary), jnp.bfloat16),
            pltpu.SemaphoreType.DMA((KEY_PIECES + 6,)),
            pltpu.SemaphoreType.DMA((2, n_devices)),
            pltpu.SemaphoreType.DMA((2, n_devices)),
            pltpu.SemaphoreType.DMA((3, KEY_PIECES + 1)),
            pltpu.SemaphoreType.DMA((3, KEY_PIECES + 1)),
            pltpu.SemaphoreType.DMA((n_chunks, QUERY_PIECES + 1)),
            pltpu.SemaphoreType.DMA((n_chunks, QUERY_PIECES + 1)),
        ],
        compiler_params=pltpu.CompilerParams(
            collective_id=0, has_side_effects=True, vmem_limit_bytes=48 * 2**20
        ),
        name="exchange",
    )(q_latent, q_gain[None, :], listed, kv_scales.T, w_uq, w_uk, latent_cache.T)


def reduce_kernel(
    query_bits, heads, cap, scale, list_ref, keys_ref, rots_ref, q_ref, q_rot_ref, out_ref, mine,
    logs, *bufs
):
    n_stages = len(query_bits)
    recvs, log_recvs = bufs[:n_stages], bufs[n_stages : 2 * n_stages]
    send_sems, recv_sems = bufs[2 * n_stages :]
    me = lax.axis_index("ctx")
    n_chunks, groups, rows, width = q_ref.shape
    n_parts = keys_ref.shape[0]
    n_batches = groups // SIDE
    total_rows = n_chunks * rows
    tokens = rows // heads
    base = 2**tokens
    span = cap * BLK
    peers = [me + bit * (1 - 2 * ((me // bit) % 2)) for bit in query_bits]
    barrier = pltpu.get_barrier_semaphore()
    for other in peers:
        pl.semaphore_signal(barrier, inc=1, device_id={"ctx": other})
    pl.semaphore_wait(barrier, n_stages)

    token_of_row = (lax.broadcasted_iota(jnp.int32, (total_rows, 1), 0) // heads) % tokens
    row_bit = lax.shift_left(jnp.ones_like(token_of_row), token_of_row)
    block_of_col = lax.broadcasted_iota(jnp.int32, (1, span), 1) // BLK
    diagonal = lax.broadcasted_iota(jnp.int32, (total_rows, total_rows), 0) == lax.broadcasted_iota(
        jnp.int32, (total_rows, total_rows), 1
    )
    transposed = (((1,), (1,)), ((), ()))

    def attend_group(batch, i):
        g = batch * SIDE + i
        query = jnp.concatenate([q_ref[c, g] for c in range(n_chunks)], axis=0)
        rotary = jnp.concatenate([q_rot_ref[c, g] for c in range(n_chunks)], axis=0)
        scores, key_rows = [], []
        for p in range(n_parts):
            entries = [list_ref[g, p * cap + k] for k in range(cap)]
            latent = jnp.concatenate([keys_ref[p, e // base] for e in entries], axis=0)
            turned = jnp.concatenate([rots_ref[p, e // base] for e in entries], axis=0)
            bits = jnp.zeros((1, span), jnp.int32)
            for k in range(cap):
                bits = jnp.where(block_of_col == k, entries[k] % base, bits)
            score = lax.dot_general(query, latent, transposed, preferred_element_type=jnp.float32)
            score = score + lax.dot_general(
                rotary, turned, transposed, preferred_element_type=jnp.float32
            )
            scores.append(jnp.where((bits & row_bit) != 0, score * scale, EMPTY))
            key_rows.append(latent)
        peak = functools.reduce(
            jnp.maximum, [jnp.max(s, axis=1, keepdims=True) for s in scores]
        )
        total = jnp.zeros_like(peak)
        value = jnp.zeros((total_rows, width), jnp.float32)
        for score, latent in zip(scores, key_rows):
            exponent = jnp.exp(score - peak)
            total = total + jnp.sum(exponent, axis=1, keepdims=True)
            value = value + jnp.dot(
                exponent.astype(jnp.bfloat16), latent, preferred_element_type=jnp.float32
            )
        value = (value / total).astype(jnp.bfloat16)
        for c in range(n_chunks):
            mine[c, g] = value[c * rows : (c + 1) * rows]
        logs[batch, pl.ds(i, 1), :] = jnp.sum(
            jnp.where(diagonal, peak + jnp.log(total), 0.0), axis=0, keepdims=True
        )

    def copies(stage, batch):
        kept = n_chunks >> (stage + 1)
        span_of = pl.ds(batch * SIDE, SIDE)
        pairs = (
            (mine.at[pl.ds(kept, kept), span_of], recvs[stage].at[:, span_of]),
            (logs.at[batch], log_recvs[stage].at[batch]),
        )
        return [
            pltpu.make_async_remote_copy(
                src_ref=source,
                dst_ref=target,
                send_sem=send_sems.at[stage, k, batch],
                recv_sem=recv_sems.at[stage, k, batch],
                device_id={"ctx": peers[stage]},
            )
            for k, (source, target) in enumerate(pairs)
        ]

    def merge(stage, batch):
        kept = n_chunks >> (stage + 1)
        for copy in copies(stage, batch):
            copy.wait()
        own = logs[batch]
        other = pltpu.roll(log_recvs[stage][batch], total_rows - kept * rows, 1)
        top = jnp.maximum(own, other)
        own_share = jnp.exp(own - top)
        other_share = jnp.exp(other - top)
        both = own_share + other_share
        own_share = own_share / both
        other_share = other_share / both
        logs[batch] = top + jnp.log(both)
        used = kept * rows

        def column(shares, i):
            return jnp.sum(
                jnp.where(diagonal[:used], shares[i : i + 1], 0.0), axis=1, keepdims=True
            )

        for i in range(SIDE):
            g = batch * SIDE + i
            left, right = column(own_share, i), column(other_share, i)
            for c in range(kept):
                part = slice(c * rows, (c + 1) * rows)
                value = (
                    mine[c, g].astype(jnp.float32) * left[part]
                    + recvs[stage][c, g].astype(jnp.float32) * right[part]
                ).astype(jnp.bfloat16)
                if stage + 1 < n_stages:
                    mine[c, g] = value
                else:
                    out_ref[g] = value

    def step(time, carry):
        for stage in reversed(range(n_stages)):
            batch = time - LAG * (stage + 1)

            @pl.when((batch >= 0) & (batch < n_batches))
            def _():
                merge(stage, batch)
                if stage + 1 < n_stages:
                    for copy in copies(stage + 1, batch):
                        copy.start()

        @pl.when(time < n_batches)
        def _():
            for i in range(SIDE):
                attend_group(time, i)
            for copy in copies(0, time):
                copy.start()

        return carry

    lax.fori_loop(0, n_batches + LAG * n_stages, step, 0)


def attend_reduce(query_bits, heads, cap, scale, block_list, keys, rots, queries, q_rots):
    n_chunks, groups, rows, width = queries.shape
    n_stages = len(query_bits)
    n_batches = groups // SIDE
    vmem = pl.BlockSpec(memory_space=pltpu.VMEM)
    smem = pl.BlockSpec(memory_space=pltpu.SMEM)
    log_shape = (n_batches, 8, n_chunks * rows)
    return pl.pallas_call(
        functools.partial(reduce_kernel, query_bits, heads, cap, scale),
        out_shape=jax.ShapeDtypeStruct((groups, rows, width), jnp.bfloat16),
        in_specs=[smem] + [vmem] * 4,
        out_specs=vmem,
        scratch_shapes=[
            pltpu.VMEM(queries.shape, jnp.bfloat16),
            pltpu.VMEM(log_shape, jnp.float32),
            *[
                pltpu.VMEM((n_chunks >> (s + 1), groups, rows, width), jnp.bfloat16)
                for s in range(n_stages)
            ],
            *[pltpu.VMEM(log_shape, jnp.float32) for _ in range(n_stages)],
            pltpu.SemaphoreType.DMA((n_stages, 2, n_batches)),
            pltpu.SemaphoreType.DMA((n_stages, 2, n_batches)),
        ],
        compiler_params=pltpu.CompilerParams(
            collective_id=2, has_side_effects=True, vmem_limit_bytes=48 * 2**20
        ),
        name="attend_reduce",
    )(block_list, keys, rots, queries, q_rots)


def project_kernel(bits, tiles, rows_ref, w_ref, out_ref, weights, w_sems, *bufs):
    n_stages = len(bits)
    sends, recvs = bufs[:n_stages], bufs[n_stages : 2 * n_stages]
    send_sems, recv_sems = bufs[2 * n_stages :]
    me = lax.axis_index("ctx")
    upper = [(me // bit) % 2 for bit in bits]
    partner = [me + bit * (1 - 2 * up) for bit, up in zip(bits, upper)]
    width = weights.shape[2]
    loads = [
        pltpu.make_async_copy(
            w_ref.at[:, pl.ds(t * width, width)], weights.at[t], w_sems.at[t]
        )
        for t in range(tiles)
    ]
    for load in loads:
        load.start()
    barrier = pltpu.get_barrier_semaphore()
    for other in partner:
        pl.semaphore_signal(barrier, inc=1, device_id={"ctx": other})
    pl.semaphore_wait(barrier, n_stages)

    def copy_of(k, t):
        return pltpu.make_async_remote_copy(
            src_ref=sends[k].at[t],
            dst_ref=recvs[k].at[t],
            send_sem=send_sems.at[t, k],
            recv_sem=recv_sems.at[t, k],
            device_id={"ctx": partner[k]},
        )

    def send_half(k, t, total):
        half = total.shape[0] // 2
        low, high = total[:half], total[half:]
        sends[k][t] = jnp.where(upper[k] == 1, low, high).astype(jnp.bfloat16)
        copy_of(k, t).start()
        return jnp.where(upper[k] == 1, high, low)

    kept = {}
    for time in range(tiles + LAG * n_stages):
        for k in reversed(range(n_stages)):
            t = time - LAG * (k + 1)
            if 0 <= t < tiles:
                copy_of(k, t).wait()
                total = kept.pop(t) + recvs[k][t].astype(jnp.float32)
                if k + 1 < n_stages:
                    kept[t] = send_half(k + 1, t, total)
                else:
                    out_ref[:, t * width : (t + 1) * width] = total.astype(jnp.bfloat16)
        if time < tiles:
            loads[time].wait()
            total = jnp.dot(rows_ref[...], weights[time], preferred_element_type=jnp.float32)
            kept[time] = send_half(0, time, total)


def project(rows, weight, q_local, n_devices):
    bits = [1 << i for i in range(n_devices.bit_length() - 1)]
    depth, columns = weight.shape
    tiles = max(t for t in range(1, TILES + 1) if columns % (t * 128) == 0)
    width = columns // tiles
    sizes = [rows.shape[0] >> (i + 1) for i in range(len(bits))]
    slots = [pltpu.VMEM((tiles, size, width), jnp.bfloat16) for size in sizes]
    vmem = pl.BlockSpec(memory_space=pltpu.VMEM)
    return pl.pallas_call(
        functools.partial(project_kernel, bits, tiles),
        out_shape=jax.ShapeDtypeStruct((q_local, columns), jnp.bfloat16),
        in_specs=[vmem, pl.BlockSpec(memory_space=pl.ANY)],
        out_specs=vmem,
        scratch_shapes=[
            pltpu.VMEM((tiles, depth, width), jnp.bfloat16),
            pltpu.SemaphoreType.DMA((tiles,)),
            *slots,
            *slots,
            pltpu.SemaphoreType.DMA((tiles, len(bits))),
            pltpu.SemaphoreType.DMA((tiles, len(bits))),
        ],
        compiler_params=pltpu.CompilerParams(
            collective_id=1, has_side_effects=True, vmem_limit_bytes=48 * 2**20
        ),
        name="project",
    )(rows, weight)


def local(
    cache_bits, query_bits, q_latent, q_gain, w_uq, w_uk, w_uv, w_o, latent_cache, kv_scales, selected, counts
):
    n_devices = lax.axis_size("ctx")
    me = lax.axis_index("ctx")
    heads_local, width_content, width_latent = w_uk.shape
    width_rotary = latent_cache.shape[1] - width_latent
    q_local, top_blocks = selected.shape
    blocks_local = latent_cache.shape[0] // BLK
    cap = q_local * top_blocks // n_devices
    groups = n_devices
    row_count = groups * q_local

    live_sel = jnp.arange(top_blocks, dtype=jnp.int32)[None, :] < counts[:, None]
    listed = jnp.where(live_sel, selected, -1)
    keys, rots, queries, q_rots, all_listed = exchange(
        cache_bits, query_bits, n_devices, q_latent, q_gain, listed, w_uq, w_uk, latent_cache, kv_scales
    )
    near_bit, far_bit = cache_bits
    parts_masks = [0, near_bit, far_bit, far_bit | near_bit]
    firsts = jnp.stack([(me ^ mask) * blocks_local for mask in parts_masks])
    held = (firsts[:, None] + jnp.arange(blocks_local, dtype=jnp.int32)[None, :]).reshape(-1)
    member = jnp.any(all_listed[:, :, :, None] == held[None, None, None, :], axis=2).astype(jnp.int32)
    bits = jnp.sum(
        member * lax.shift_left(1, jnp.arange(q_local, dtype=jnp.int32))[None, :, None], axis=1
    ).reshape(groups, len(parts_masks), blocks_local)
    needed = (bits > 0).astype(jnp.int32)
    rank = jnp.cumsum(needed, axis=2) - needed
    entry = jnp.arange(blocks_local, dtype=jnp.int32)[None, None, :] * 2**q_local + bits
    slots = jnp.arange(cap, dtype=jnp.int32)[None, None, :, None]
    slot = (rank[:, :, None, :] == slots) & (needed[:, :, None, :] == 1)
    block_list = jnp.sum(jnp.where(slot, entry[:, :, None, :], 0), axis=3).reshape(groups, -1)

    scale = 1.0 / math.sqrt(width_content + width_rotary)
    latent_out = attend_reduce(
        query_bits, heads_local, cap, scale, block_list, keys, rots, queries, q_rots
    )
    head_out = latent_out.reshape(row_count, heads_local, width_latent)
    head_values = jnp.einsum(
        "qhc,hcv->qhv", head_out, w_uv, preferred_element_type=jnp.float32
    ).astype(jnp.bfloat16)
    n_bits = n_devices.bit_length() - 1
    rows = head_values.reshape((2,) * n_bits + (q_local, -1))
    rows = rows.transpose(tuple(reversed(range(n_bits))) + (n_bits, n_bits + 1))
    return project(rows.reshape(row_count, -1), w_o, q_local, n_devices)


def solution(mesh):
    n_devices = mesh.shape["ctx"]
    all_bits = [1 << i for i in range(n_devices.bit_length() - 1)]
    cache_bits, query_bits = all_bits[:2], all_bits[2:]
    in_specs = (
        P(("groups", "ctx"), None),
        P(),
        P(None, "ctx"),
        P("ctx", None, None),
        P("ctx", None, None),
        P("ctx", None),
        P(("groups", "ctx"), None),
        P(("groups", "ctx"), None),
        P(("groups", "ctx"), None),
        P(("groups", "ctx")),
    )
    out_specs = P(("groups", "ctx"), None)
    return jax.shard_map(
        functools.partial(local, cache_bits, query_bits),
        mesh=mesh,
        in_specs=in_specs,
        out_specs=out_specs,
        check_vma=False,
    )
```

time: 191 us -> 152 us (0.80)
  waiting for transfers between devices: 85.2 us -> 0 us
  Pallas kernels: 61 us -> 139 us
  starting transfers between devices: 25.2 us -> 0 us
  other arithmetic: 9.01 us -> 3.42 us
  matrix products: 4.05 us -> 0.38 us
  local copies, waits for them, and re-layouts: 7.08 us -> 9.43 us
    ppermute x14 -> x0, waiting for transfers between devices: 85.2 us -> none  [xor_permute(): lax.ppermute(value, 'ctx', [(i, i ^ distance) for i in range(n_devices)])]
    pallas_call x2, Pallas kernels: 37.7 us -> 117 us  [the longest x1 66.8 us: exchange(): pl.pallas_call(functools.partial(exchange_kernel, cache_bits, query_bits)...]
    ppermute x14 -> x0, starting transfers between devices: 25.2 us -> none  [xor_permute(): lax.ppermute(value, 'ctx', [(i, i ^ distance) for i in range(n_devices)])]
    unnamed x5 -> x17, local copies, waits for them, and re-layouts: 0.64 us -> 8.18 us
    convert_element_type x7 -> x0, other arithmetic: 4.31 us -> none  [the longest x1 2.08 us: local(): scaled_t = (cache_t[:width_latent].astype(jnp.float32).reshape(tiles, wid...]
    dot_general x2 -> x0, matrix products: 3.67 us -> none  [the longest x1 3.38 us: local(): jnp.dot(all_normed, w_uq, preferred_element_type=jnp.float32)]
    transpose x2 -> x0, local copies, waits for them, and re-layouts: 2.15 us -> none  [local(): x.T.reshape(piece_blocks, BLK, width_row)]
  transfers between devices with their start and end apart: 14 -> 0, of which waited for: 7 -> 0; matrix products, arithmetic and copies ran while one was open for 4% -> 0% of each run, Pallas kernels for 0% -> 0%
where the time goes in v1:
time: 152 us
  Pallas kernels  139 us (91%)
  local copies, waits for them, and re-layouts  9.43 us (6%)
  other arithmetic  3.42 us (2%)
    pallas_call x1, Pallas kernels, exchange(): pl.pallas_call(functools.partial(exchange_kernel, cache_bits, query_bits)...  66.8 us
    pallas_call x1, Pallas kernels, attend_reduce(): pl.pallas_call(functools.partial(reduce_kernel, query_bits, heads, cap, s...  49.8 us
    pallas_call x1, Pallas kernels, project(): pl.pallas_call(functools.partial(project_kernel, bits, tiles), out_shape=...  22.1 us
    unnamed x17, local copies, waits for them, and re-layouts  8.18 us

profile of v1, /device:TPU:0, one launch (start us, length us, event | category | flops | bytes accessed | tf_op | source)
XLA Modules:
  0.0 152.0 jit_solution(15139834998887562826)
XLA Ops:
  0.0 0.0 copy-start
  0.0 0.1 pad_add_fusion
  0.1 0.1 iota_add_fusion
  0.2 0.1 add.32
  0.2 0.8 fusion.4.sel_ref
  1.1 0.7 broadcast_in_dim.14.gain_ref
  1.8 0.0 copy-start.3
  1.8 1.2 copy-done.3
  3.0 0.0 copy-start.6
  3.0 0.8 copy-done.6
  3.8 0.0 copy-start.7
  3.8 0.7 copy-done.7
  4.5 66.8 %exchange.1 = (bf16[4,32,64,512]{3,2,1,0:T(8,128)(2,1)}, bf16[4,32,64,128]{3,2,1,0:T(8,128)(2,1)S(1)}, bf16[4,16,32,512]{3,2,1,0:T(8,128)(2,1)S(1)}, bf16[4,16,3...) custom-call(bf16[4,1536]{1,0:T(4,128)(2,1)S(1)} %copy-done.7, f32[1,1536]{1,0:T(1,128)S(1)} %broadcast_in_dim.14.gain_ref, ...), custom_call_target="tpu_custom_call" | custom-call | tf_op jit(solution)/shard_map/exchange/pallas_call | solution.py:264
  71.2 0.0 copy-start.1
  71.2 1.4 copy-done.1
  72.6 0.0 copy-start.4
  72.6 0.8 copy-done.4
  73.4 0.4 compare_reduce_fusion
  73.8 0.1 select_reduce_fusion.1
  73.9 0.1 reshape.69
  74.1 0.8 reduce_window_sum.11
  74.9 1.2 select_reduce_fusion
  76.0 0.1 copy.26
  76.1 0.1 copy.27.list_ref
  76.2 0.0 copy-start.2
  76.2 1.6 %copy-done.2 = bf16[4,16,32,512]{3,2,1,0:T(8,128)(2,1)S(1)} copy-done((bf16[4,16,32,512]{3,2,1,0:T(8,128)(2,1)S(1)}, bf16[4,16,32,512]{3,2,1,0:T(8,128)(2,1)}, u32[]{:S(2)}) %copy-start.2) | copy-done | bytes 2097176
  77.8 0.0 copy-start.5
  77.8 1.0 copy-done.5
  78.8 49.8 %attend_reduce.1 = bf16[16,32,512]{2,1,0:T(8,128)(2,1)S(1)} custom-call(s32[16,32]{1,0:T(8,128)S(1)} %copy.27.list_ref, bf16[4,32,64,512]{3,2,1,0:T(8,128)(2,1)} %get-tuple-element.11.keys_ref, bf16[4,32,64,128]{3,2,1,0:T(8,128)(2,1)S(1)} %get-tuple-element.12.rots_ref, bf16[4,16,32,512]{3,2,1,0:T(8,128)(2,1)S(1)} %copy-done.2, ...), custom_call_target="tpu_custom_call" | custom-call | tf_op jit(solution)/shard_map/attend_reduce/pallas_call | solution.py:450
  128.6 0.0 copy-done
  128.6 0.4 fusion
  129.0 0.1 copy.29
  129.2 22.1 %project.1 = bf16[4,7168]{1,0:T(4,128)(2,1)S(1)} custom-call(bf16[64,1024]{1,0:T(8,128)(2,1)S(1)} %reshape.73.rows_ref, bf16[1024,7168]{1,0:T(8,128)(2,1)} %w_ref.1), custom_call_target="tpu_custom_call" | custom-call | tf_op jit(solution)/shard_map/project/pallas_call | solution.py:535
  151.4 0.6 copy.42
  (10 shorter events, 0.2 us)
Async XLA Ops:
  0.0 128.6 %copy-start = (bf16[8,512,128]{2,1,0:T(8,128)(2,1)S(1)}, bf16[8,512,128]{2,1,0:T(8,128)(2,1)}, u32[]{:S(2)}) copy-start(bf16[8,512,128]{2,1,0:T(8,128)(2,1)} %param.14) | copy-start | bytes 3145732
  1.8 1.2 copy-start.3
  3.0 0.8 copy-start.6
  3.8 0.7 copy-start.7
  71.2 1.4 copy-start.1
  72.6 0.8 copy-start.4
  76.2 1.6 %copy-start.2 = (bf16[4,16,32,512]{3,2,1,0:T(8,128)(2,1)S(1)}, bf16[4,16,32,512]{3,2,1,0:T(8,128)(2,1)}, u32[]{:S(2)}) copy-start(bf16[4,16,32,512]{3,2,1,0:T(8,128)(2,1)} %copy-done.1) | copy-start | bytes 6291460
  77.8 1.0 copy-start.5

commit v2 on v1

--- a/solution.py
+++ b/solution.py
@@ -10,8 +10,9 @@
 
 BLK = 64
 SIDE = 2
-TILES = 7
+TILES = 4
 LAG = 2
+SUM_LAG = 2
 KEY_PIECES = 8
 QUERY_PIECES = 4
 
@@ -20,11 +21,189 @@
 EMPTY = -1e30
 
 
-def exchange_kernel(
-    cache_bits, query_bits, q_ref, gain_ref, sel_ref, scales_ref, w_uq_ref, w_uk_ref, cache_ref,
-    keys_ref, rots_ref, q_out_ref, q_rot_ref, sel_out_ref, q_in, gain, scales, raw, w_uq, w_uk,
-    normed, lat, rows_x, rows_q, rows_r, q_pack, load_sems, gather_send, gather_recv, key_send,
-    key_recv, q_send, q_recv,
+def make_list(owners, cap, blocks, q_local, listed_ref, list_rows):
+    total = listed_ref.shape[0]
+    groups = math.gcd(total, 16)
+
+    def some_groups(i, carry):
+        some = pl.ds(i * groups, groups)
+        width = len(owners) * blocks
+        lane = lax.broadcasted_iota(jnp.int32, (groups, width), 1)
+        inner = lane % blocks
+        held = inner
+        for p, owner in enumerate(owners):
+            held = held + jnp.where(lane // blocks == p, owner * blocks, 0)
+        bits = jnp.zeros((groups, width), jnp.int32)
+        for t in range(q_local):
+            listed = listed_ref[some, t, :]
+            member = jnp.zeros((groups, width), jnp.int32)
+            for k in range(listed.shape[1]):
+                member = jnp.where(listed[:, k : k + 1] == held, 2**t, member)
+            bits = bits + member
+        needed = jnp.where(bits > 0, 1, 0)
+        upto = needed
+        reach = 1
+        while reach < blocks:
+            upto = upto + jnp.where(inner >= reach, pltpu.roll(upto, reach, 1), 0)
+            reach *= 2
+        rank = upto - needed
+        entry = inner * 2**q_local + bits
+        result = jnp.zeros((groups, width), jnp.int32)
+        for r in range(cap):
+            found = jnp.where((rank == r) & (needed == 1), entry, 0)
+            reach = blocks // 2
+            while reach:
+                found = found + pltpu.roll(found, width - reach, 1)
+                reach //= 2
+            if r:
+                found = pltpu.roll(found, r, 1)
+            result = jnp.where(inner == r, found, result)
+        list_rows[some, :] = result
+        return carry
+
+    lax.fori_loop(0, total // groups, some_groups, 0)
+
+
+def attend_reduce(
+    query_bits, heads, cap, scale, list_ref, keys_ref, rots_ref, q_ref, q_rot_ref, out_ref, mine,
+    logs, *bufs
+):
+    n_stages = len(query_bits)
+    recvs, log_recvs = bufs[:n_stages], bufs[n_stages : 2 * n_stages]
+    send_sems, recv_sems = bufs[2 * n_stages :]
+    me = lax.axis_index("ctx")
+    n_chunks, groups, rows, width = q_ref.shape
+    n_parts = keys_ref.shape[0]
+    n_batches = groups // SIDE
+    total_rows = n_chunks * rows
+    tokens = rows // heads
+    base = 2**tokens
+    span = cap * BLK
+    peers = [me + bit * (1 - 2 * ((me // bit) % 2)) for bit in query_bits]
+    token_of_row = (lax.broadcasted_iota(jnp.int32, (total_rows, 1), 0) // heads) % tokens
+    row_bit = lax.shift_left(jnp.ones_like(token_of_row), token_of_row)
+    block_of_col = lax.broadcasted_iota(jnp.int32, (1, span), 1) // BLK
+    diagonal = lax.broadcasted_iota(jnp.int32, (total_rows, total_rows), 0) == lax.broadcasted_iota(
+        jnp.int32, (total_rows, total_rows), 1
+    )
+    transposed = (((1,), (1,)), ((), ()))
+
+    def attend_group(batch, i):
+        g = batch * SIDE + i
+        query = jnp.concatenate([q_ref[c, g] for c in range(n_chunks)], axis=0)
+        rotary = jnp.concatenate([q_rot_ref[c, g] for c in range(n_chunks)], axis=0)
+        scores, key_rows = [], []
+        for p in range(n_parts):
+            entries = [list_ref[g, p * keys_ref.shape[1] + k] for k in range(cap)]
+            latent = jnp.concatenate([keys_ref[p, e // base] for e in entries], axis=0)
+            turned = jnp.concatenate([rots_ref[p, e // base] for e in entries], axis=0)
+            bits = jnp.zeros((1, span), jnp.int32)
+            for k in range(cap):
+                bits = jnp.where(block_of_col == k, entries[k] % base, bits)
+            score = lax.dot_general(query, latent, transposed, preferred_element_type=jnp.float32)
+            score = score + lax.dot_general(
+                rotary, turned, transposed, preferred_element_type=jnp.float32
+            )
+            scores.append(jnp.where((bits & row_bit) != 0, score * scale, EMPTY))
+            key_rows.append(latent)
+        peak = functools.reduce(
+            jnp.maximum, [jnp.max(s, axis=1, keepdims=True) for s in scores]
+        )
+        total = jnp.zeros_like(peak)
+        value = jnp.zeros((total_rows, width), jnp.float32)
+        for score, latent in zip(scores, key_rows):
+            exponent = jnp.exp(score - peak)
+            total = total + jnp.sum(exponent, axis=1, keepdims=True)
+            value = value + jnp.dot(
+                exponent.astype(jnp.bfloat16), latent, preferred_element_type=jnp.float32
+            )
+        value = (value / total).astype(jnp.bfloat16)
+        for c in range(n_chunks):
+            mine[c, g] = value[c * rows : (c + 1) * rows]
+        logs[batch, pl.ds(i, 1), :] = jnp.sum(
+            jnp.where(diagonal, peak + jnp.log(total), 0.0), axis=0, keepdims=True
+        )
+
+    def copies(stage, batch):
+        kept = n_chunks >> (stage + 1)
+        span_of = pl.ds(batch * SIDE, SIDE)
+        pairs = (
+            (mine.at[pl.ds(kept, kept), span_of], recvs[stage].at[:, span_of]),
+            (logs.at[batch], log_recvs[stage].at[batch]),
+        )
+        return [
+            pltpu.make_async_remote_copy(
+                src_ref=source,
+                dst_ref=target,
+                send_sem=send_sems.at[stage, k, batch],
+                recv_sem=recv_sems.at[stage, k, batch],
+                device_id={"ctx": peers[stage]},
+            )
+            for k, (source, target) in enumerate(pairs)
+        ]
+
+    def merge(stage, batch):
+        kept = n_chunks >> (stage + 1)
+        for copy in copies(stage, batch):
+            copy.wait()
+        own = logs[batch]
+        other = pltpu.roll(log_recvs[stage][batch], total_rows - kept * rows, 1)
+        top = jnp.maximum(own, other)
+        own_share = jnp.exp(own - top)
+        other_share = jnp.exp(other - top)
+        both = own_share + other_share
+        own_share = own_share / both
+        other_share = other_share / both
+        logs[batch] = top + jnp.log(both)
+        used = kept * rows
+
+        def column(shares, i):
+            return jnp.sum(
+                jnp.where(diagonal[:used], shares[i : i + 1], 0.0), axis=1, keepdims=True
+            )
+
+        for i in range(SIDE):
+            g = batch * SIDE + i
+            left, right = column(own_share, i), column(other_share, i)
+            for c in range(kept):
+                part = slice(c * rows, (c + 1) * rows)
+                value = (
+                    mine[c, g].astype(jnp.float32) * left[part]
+                    + recvs[stage][c, g].astype(jnp.float32) * right[part]
+                ).astype(jnp.bfloat16)
+                if stage + 1 < n_stages:
+                    mine[c, g] = value
+                else:
+                    out_ref[g] = value
+
+    def step(time, carry):
+        for stage in reversed(range(n_stages)):
+            batch = time - LAG * (stage + 1)
+
+            @pl.when((batch >= 0) & (batch < n_batches))
+            def _():
+                merge(stage, batch)
+                if stage + 1 < n_stages:
+                    for copy in copies(stage + 1, batch):
+                        copy.start()
+
+        @pl.when(time < n_batches)
+        def _():
+            for i in range(SIDE):
+                attend_group(time, i)
+            for copy in copies(0, time):
+                copy.start()
+
+        return carry
+
+    lax.fori_loop(0, n_batches + LAG * n_stages, step, 0)
+
+
+def attend_kernel(
+    cache_bits, query_bits, cap, scale, q_ref, gain_ref, sel_ref, scales_ref, w_uq_ref, w_uk_ref,
+    cache_ref, out_ref, keys_ref, rots_ref, q_out_ref, q_rot_ref, sel_out_ref, q_in, gain, scales,
+    raw, w_uq, w_uk, normed, lat, rows_x, rows_q, rows_r, q_pack, list_rows, list_ref,
+    load_sems, gather_send, gather_recv, key_send, key_recv, q_send, q_recv, *reduce_refs,
 ):
     n_devices = lat.shape[0]
     me = lax.axis_index("ctx")
@@ -209,6 +388,10 @@
         rolled = jnp.concatenate([pair[:, :, width_rotary:], pair[:, :, :width_rotary]], axis=2)
         rots_ref[slot, blocks // 2 :] = rolled.astype(jnp.bfloat16)
 
+    owners = [me, peer(near_bit), peer(far_bit), peer(near_bit) + peer(far_bit) - me]
+    make_list(owners, cap, blocks, q_local, sel_out_ref, list_rows)
+    list_load = pltpu.make_async_copy(list_rows, list_ref, load_sems.at[KEY_PIECES + 6])
+    list_load.start()
     unpack_query(0)
     unpack_rots(0)
     key_copy(0, KEY_PIECES).wait_recv()
@@ -235,10 +418,15 @@
                 unpack_query(a)
     key_copy(2, KEY_PIECES).wait_recv()
     unpack_rots(3)
+    for i in range(KEY_PIECES):
+        key_copy(0, i).wait_recv()
+        key_copy(2, i).wait_recv()
+    list_load.wait()
+    attend_reduce(
+        query_bits, heads, cap, scale, list_ref, keys_ref, rots_ref, q_out_ref, q_rot_ref, out_ref,
+        *reduce_refs
+    )
     for i in range(KEY_PIECES + 1):
-        if i < KEY_PIECES:
-            key_copy(0, i).wait_recv()
-            key_copy(2, i).wait_recv()
         for kind in range(3):
             key_copy(kind, i).wait_send()
     for j in range(QUERY_PIECES + 1):
@@ -247,8 +435,9 @@
             q_copy(stage, slot - 2**stage, j).wait_send()
 
 
-def exchange(
-    cache_bits, query_bits, n_devices, q_latent, q_gain, listed, w_uq, w_uk, latent_cache, kv_scales
+def attend(
+    cache_bits, query_bits, cap, scale, n_devices, q_latent, q_gain, listed, w_uq, w_uk, latent_cache,
+    kv_scales
 ):
     q_local, width_q = q_latent.shape
     heads, _, width_latent = w_uk.shape
@@ -256,23 +445,26 @@
     blocks = span // BLK
     tokens = n_devices * q_local
     groups = n_devices
-    n_chunks = 2 ** len(query_bits)
+    n_stages = len(query_bits)
+    n_chunks = 2**n_stages
     rows = q_local * heads
     width_rotary = width_row - width_latent
+    n_batches = groups // SIDE
+    log_shape = (n_batches, 8, n_chunks * rows)
     vmem = pl.BlockSpec(memory_space=pltpu.VMEM)
     any_space = pl.BlockSpec(memory_space=pl.ANY)
+    half_keys = pltpu.VMEM((4, blocks, BLK, 2 * width_rotary), jnp.bfloat16)
     return pl.pallas_call(
-        functools.partial(exchange_kernel, cache_bits, query_bits),
-        out_shape=[
-            jax.ShapeDtypeStruct((4, blocks, BLK, width_latent), jnp.bfloat16),
-            jax.ShapeDtypeStruct((4, blocks, BLK, 2 * width_rotary), jnp.bfloat16),
-            jax.ShapeDtypeStruct((n_chunks, groups, rows, width_latent), jnp.bfloat16),
-            jax.ShapeDtypeStruct((n_chunks, groups, rows, 2 * width_rotary), jnp.bfloat16),
-            jax.ShapeDtypeStruct((n_devices,) + listed.shape, jnp.int32),
-        ],
+        functools.partial(attend_kernel, cache_bits, query_bits, cap, scale),
+        out_shape=jax.ShapeDtypeStruct((groups, rows, width_latent), jnp.bfloat16),
         in_specs=[any_space] * 2 + [vmem] + [any_space] * 4,
-        out_specs=[vmem] * 5,
+        out_specs=vmem,
         scratch_shapes=[
+            pltpu.VMEM((4, blocks, BLK, width_latent), jnp.bfloat16),
+            half_keys,
+            pltpu.VMEM((n_chunks, groups, rows, width_latent), jnp.bfloat16),
+            pltpu.VMEM((n_chunks, groups, rows, 2 * width_rotary), jnp.bfloat16),
+            pltpu.VMEM((n_devices,) + listed.shape, jnp.int32),
             pltpu.VMEM(q_latent.shape, jnp.bfloat16),
             pltpu.VMEM((1, width_q), jnp.float32),
             pltpu.VMEM(kv_scales.shape[::-1], jnp.float32),
@@ -285,178 +477,19 @@
             pltpu.VMEM((tokens, heads, width_latent), jnp.float32),
             pltpu.VMEM((tokens, heads, width_rotary), jnp.float32),
             pltpu.VMEM((n_chunks, groups // 2, rows, 2 * width_rotary), jnp.bfloat16),
-            pltpu.SemaphoreType.DMA((KEY_PIECES + 6,)),
+            pltpu.VMEM((groups, 4 * blocks), jnp.int32),
+            pltpu.SMEM((groups, 4 * blocks), jnp.int32),
+            pltpu.SemaphoreType.DMA((KEY_PIECES + 7,)),
             pltpu.SemaphoreType.DMA((2, n_devices)),
             pltpu.SemaphoreType.DMA((2, n_devices)),
             pltpu.SemaphoreType.DMA((3, KEY_PIECES + 1)),
             pltpu.SemaphoreType.DMA((3, KEY_PIECES + 1)),
             pltpu.SemaphoreType.DMA((n_chunks, QUERY_PIECES + 1)),
             pltpu.SemaphoreType.DMA((n_chunks, QUERY_PIECES + 1)),
-        ],
-        compiler_params=pltpu.CompilerParams(
-            collective_id=0, has_side_effects=True, vmem_limit_bytes=48 * 2**20
-        ),
-        name="exchange",
-    )(q_latent, q_gain[None, :], listed, kv_scales.T, w_uq, w_uk, latent_cache.T)
-
-
-def reduce_kernel(
-    query_bits, heads, cap, scale, list_ref, keys_ref, rots_ref, q_ref, q_rot_ref, out_ref, mine,
-    logs, *bufs
-):
-    n_stages = len(query_bits)
-    recvs, log_recvs = bufs[:n_stages], bufs[n_stages : 2 * n_stages]
-    send_sems, recv_sems = bufs[2 * n_stages :]
-    me = lax.axis_index("ctx")
-    n_chunks, groups, rows, width = q_ref.shape
-    n_parts = keys_ref.shape[0]
-    n_batches = groups // SIDE
-    total_rows = n_chunks * rows
-    tokens = rows // heads
-    base = 2**tokens
-    span = cap * BLK
-    peers = [me + bit * (1 - 2 * ((me // bit) % 2)) for bit in query_bits]
-    barrier = pltpu.get_barrier_semaphore()
-    for other in peers:
-        pl.semaphore_signal(barrier, inc=1, device_id={"ctx": other})
-    pl.semaphore_wait(barrier, n_stages)
-
-    token_of_row = (lax.broadcasted_iota(jnp.int32, (total_rows, 1), 0) // heads) % tokens
-    row_bit = lax.shift_left(jnp.ones_like(token_of_row), token_of_row)
-    block_of_col = lax.broadcasted_iota(jnp.int32, (1, span), 1) // BLK
-    diagonal = lax.broadcasted_iota(jnp.int32, (total_rows, total_rows), 0) == lax.broadcasted_iota(
-        jnp.int32, (total_rows, total_rows), 1
-    )
-    transposed = (((1,), (1,)), ((), ()))
-
-    def attend_group(batch, i):
-        g = batch * SIDE + i
-        query = jnp.concatenate([q_ref[c, g] for c in range(n_chunks)], axis=0)
-        rotary = jnp.concatenate([q_rot_ref[c, g] for c in range(n_chunks)], axis=0)
-        scores, key_rows = [], []
-        for p in range(n_parts):
-            entries = [list_ref[g, p * cap + k] for k in range(cap)]
-            latent = jnp.concatenate([keys_ref[p, e // base] for e in entries], axis=0)
-            turned = jnp.concatenate([rots_ref[p, e // base] for e in entries], axis=0)
-            bits = jnp.zeros((1, span), jnp.int32)
-            for k in range(cap):
-                bits = jnp.where(block_of_col == k, entries[k] % base, bits)
-            score = lax.dot_general(query, latent, transposed, preferred_element_type=jnp.float32)
-            score = score + lax.dot_general(
-                rotary, turned, transposed, preferred_element_type=jnp.float32
-            )
-            scores.append(jnp.where((bits & row_bit) != 0, score * scale, EMPTY))
-            key_rows.append(latent)
-        peak = functools.reduce(
-            jnp.maximum, [jnp.max(s, axis=1, keepdims=True) for s in scores]
-        )
-        total = jnp.zeros_like(peak)
-        value = jnp.zeros((total_rows, width), jnp.float32)
-        for score, latent in zip(scores, key_rows):
-            exponent = jnp.exp(score - peak)
-            total = total + jnp.sum(exponent, axis=1, keepdims=True)
-            value = value + jnp.dot(
-                exponent.astype(jnp.bfloat16), latent, preferred_element_type=jnp.float32
-            )
-        value = (value / total).astype(jnp.bfloat16)
-        for c in range(n_chunks):
-            mine[c, g] = value[c * rows : (c + 1) * rows]
-        logs[batch, pl.ds(i, 1), :] = jnp.sum(
-            jnp.where(diagonal, peak + jnp.log(total), 0.0), axis=0, keepdims=True
-        )
-
-    def copies(stage, batch):
-        kept = n_chunks >> (stage + 1)
-        span_of = pl.ds(batch * SIDE, SIDE)
-        pairs = (
-            (mine.at[pl.ds(kept, kept), span_of], recvs[stage].at[:, span_of]),
-            (logs.at[batch], log_recvs[stage].at[batch]),
-        )
-        return [
-            pltpu.make_async_remote_copy(
-                src_ref=source,
-                dst_ref=target,
-                send_sem=send_sems.at[stage, k, batch],
-                recv_sem=recv_sems.at[stage, k, batch],
-                device_id={"ctx": peers[stage]},
-            )
-            for k, (source, target) in enumerate(pairs)
-        ]
-
-    def merge(stage, batch):
-        kept = n_chunks >> (stage + 1)
-        for copy in copies(stage, batch):
-            copy.wait()
-        own = logs[batch]
-        other = pltpu.roll(log_recvs[stage][batch], total_rows - kept * rows, 1)
-        top = jnp.maximum(own, other)
-        own_share = jnp.exp(own - top)
-        other_share = jnp.exp(other - top)
-        both = own_share + other_share
-        own_share = own_share / both
-        other_share = other_share / both
-        logs[batch] = top + jnp.log(both)
-        used = kept * rows
-
-        def column(shares, i):
-            return jnp.sum(
-                jnp.where(diagonal[:used], shares[i : i + 1], 0.0), axis=1, keepdims=True
-            )
-
-        for i in range(SIDE):
-            g = batch * SIDE + i
-            left, right = column(own_share, i), column(other_share, i)
-            for c in range(kept):
-                part = slice(c * rows, (c + 1) * rows)
-                value = (
-                    mine[c, g].astype(jnp.float32) * left[part]
-                    + recvs[stage][c, g].astype(jnp.float32) * right[part]
-                ).astype(jnp.bfloat16)
-                if stage + 1 < n_stages:
-                    mine[c, g] = value
-                else:
-                    out_ref[g] = value
-
-    def step(time, carry):
-        for stage in reversed(range(n_stages)):
-            batch = time - LAG * (stage + 1)
-
-            @pl.when((batch >= 0) & (batch < n_batches))
-            def _():
-                merge(stage, batch)
-                if stage + 1 < n_stages:
-                    for copy in copies(stage + 1, batch):
-                        copy.start()
-
-        @pl.when(time < n_batches)
-        def _():
-            for i in range(SIDE):
-                attend_group(time, i)
-            for copy in copies(0, time):
-                copy.start()
-
-        return carry
-
-    lax.fori_loop(0, n_batches + LAG * n_stages, step, 0)
-
-
-def attend_reduce(query_bits, heads, cap, scale, block_list, keys, rots, queries, q_rots):
-    n_chunks, groups, rows, width = queries.shape
-    n_stages = len(query_bits)
-    n_batches = groups // SIDE
-    vmem = pl.BlockSpec(memory_space=pltpu.VMEM)
-    smem = pl.BlockSpec(memory_space=pltpu.SMEM)
-    log_shape = (n_batches, 8, n_chunks * rows)
-    return pl.pallas_call(
-        functools.partial(reduce_kernel, query_bits, heads, cap, scale),
-        out_shape=jax.ShapeDtypeStruct((groups, rows, width), jnp.bfloat16),
-        in_specs=[smem] + [vmem] * 4,
-        out_specs=vmem,
-        scratch_shapes=[
-            pltpu.VMEM(queries.shape, jnp.bfloat16),
+            pltpu.VMEM((n_chunks, groups, rows, width_latent), jnp.bfloat16),
             pltpu.VMEM(log_shape, jnp.float32),
             *[
-                pltpu.VMEM((n_chunks >> (s + 1), groups, rows, width), jnp.bfloat16)
+                pltpu.VMEM((n_chunks >> (s + 1), groups, rows, width_latent), jnp.bfloat16)
                 for s in range(n_stages)
             ],
             *[pltpu.VMEM(log_shape, jnp.float32) for _ in range(n_stages)],
@@ -464,10 +497,10 @@
             pltpu.SemaphoreType.DMA((n_stages, 2, n_batches)),
         ],
         compiler_params=pltpu.CompilerParams(
-            collective_id=2, has_side_effects=True, vmem_limit_bytes=48 * 2**20
+            collective_id=0, has_side_effects=True, vmem_limit_bytes=58 * 2**20
         ),
-        name="attend_reduce",
-    )(block_list, keys, rots, queries, q_rots)
+        name="attend",
+    )(q_latent, q_gain[None, :], listed, kv_scales.T, w_uq, w_uk, latent_cache.T)
 
 
 def project_kernel(bits, tiles, rows_ref, w_ref, out_ref, weights, w_sems, *bufs):
@@ -508,9 +541,9 @@
         return jnp.where(upper[k] == 1, high, low)
 
     kept = {}
-    for time in range(tiles + LAG * n_stages):
+    for time in range(tiles + SUM_LAG * n_stages):
         for k in reversed(range(n_stages)):
-            t = time - LAG * (k + 1)
+            t = time - SUM_LAG * (k + 1)
             if 0 <= t < tiles:
                 copy_of(k, t).wait()
                 total = kept.pop(t) + recvs[k][t].astype(jnp.float32)
@@ -556,38 +589,18 @@
     cache_bits, query_bits, q_latent, q_gain, w_uq, w_uk, w_uv, w_o, latent_cache, kv_scales, selected, counts
 ):
     n_devices = lax.axis_size("ctx")
-    me = lax.axis_index("ctx")
     heads_local, width_content, width_latent = w_uk.shape
     width_rotary = latent_cache.shape[1] - width_latent
     q_local, top_blocks = selected.shape
-    blocks_local = latent_cache.shape[0] // BLK
     cap = q_local * top_blocks // n_devices
-    groups = n_devices
-    row_count = groups * q_local
+    row_count = n_devices * q_local
 
     live_sel = jnp.arange(top_blocks, dtype=jnp.int32)[None, :] < counts[:, None]
     listed = jnp.where(live_sel, selected, -1)
-    keys, rots, queries, q_rots, all_listed = exchange(
-        cache_bits, query_bits, n_devices, q_latent, q_gain, listed, w_uq, w_uk, latent_cache, kv_scales
-    )
-    near_bit, far_bit = cache_bits
-    parts_masks = [0, near_bit, far_bit, far_bit | near_bit]
-    firsts = jnp.stack([(me ^ mask) * blocks_local for mask in parts_masks])
-    held = (firsts[:, None] + jnp.arange(blocks_local, dtype=jnp.int32)[None, :]).reshape(-1)
-    member = jnp.any(all_listed[:, :, :, None] == held[None, None, None, :], axis=2).astype(jnp.int32)
-    bits = jnp.sum(
-        member * lax.shift_left(1, jnp.arange(q_local, dtype=jnp.int32))[None, :, None], axis=1
-    ).reshape(groups, len(parts_masks), blocks_local)
-    needed = (bits > 0).astype(jnp.int32)
-    rank = jnp.cumsum(needed, axis=2) - needed
-    entry = jnp.arange(blocks_local, dtype=jnp.int32)[None, None, :] * 2**q_local + bits
-    slots = jnp.arange(cap, dtype=jnp.int32)[None, None, :, None]
-    slot = (rank[:, :, None, :] == slots) & (needed[:, :, None, :] == 1)
-    block_list = jnp.sum(jnp.where(slot, entry[:, :, None, :], 0), axis=3).reshape(groups, -1)
-
     scale = 1.0 / math.sqrt(width_content + width_rotary)
-    latent_out = attend_reduce(
-        query_bits, heads_local, cap, scale, block_list, keys, rots, queries, q_rots
+    latent_out = attend(
+        cache_bits, query_bits, cap, scale, n_devices, q_latent, q_gain, listed, w_uq, w_uk,
+        latent_cache, kv_scales
     )
     head_out = latent_out.reshape(row_count, heads_local, width_latent)
     head_values = jnp.einsum(

time: 152 us -> 133 us (0.88)
  Pallas kernels: 139 us -> 128 us
  local copies, waits for them, and re-layouts: 9.43 us -> 2.13 us
  other arithmetic: 3.42 us -> 1.42 us
    pallas_call x2 -> x1, Pallas kernels: 117 us -> 109 us  [attend(): pl.pallas_call(functools.partial(attend_kernel, cache_bits, query_bits, c...]
    unnamed x17 -> x3, local copies, waits for them, and re-layouts: 8.18 us -> 0.63 us
    pallas_call x1, Pallas kernels: 22.1 us -> 18.7 us  [project(): pl.pallas_call(functools.partial(project_kernel, bits, tiles), out_shape=...]
where the time goes in v2:
time: 133 us
  Pallas kernels  128 us (96%)
  local copies, waits for them, and re-layouts  2.13 us (2%)
  other arithmetic  1.42 us (1%)
  matrix products  1.42 us (1%)
    pallas_call x1, Pallas kernels, attend(): pl.pallas_call(functools.partial(attend_kernel, cache_bits, query_bits, c...  109 us
    pallas_call x1, Pallas kernels, project(): pl.pallas_call(functools.partial(project_kernel, bits, tiles), out_shape=...  18.7 us

profile of v2, /device:TPU:0, one launch (start us, length us, event | category | flops | bytes accessed | tf_op | source)
XLA Modules:
  0.0 132.6 jit_solution(2608344245167511707)
XLA Ops:
  0.0 0.0 copy-start
  0.0 1.4 %fusion.2.sel_ref = s32[4,32]{1,0:T(4,128)} fusion(s32[4,32]{1,0:T(4,128)} %param.18, s32[4]{0:T(128)} %param.19), kind=kLoop, calls=%fused_computation.4 | loop fusion | flops 256 | bytes 1040 | tf_op jit(solution)/shard_map/jit(_where)/select_n | solution.py:599
  1.4 1.3 broadcast_in_dim.9.gain_ref
  2.7 108.9 %attend.1 = bf16[16,32,512]{2,1,0:T(8,128)(2,1)} custom-call(bf16[4,1536]{1,0:T(4,128)(2,1)} %q_ref.1, f32[1,1536]{1,0:T(1,128)} %broadcast_in_dim.9.gain_ref, s32[4,32]{1,0:T(4,128)} %fusion.2.sel_ref, f32[4,2048]{1,0:T(4,128)} %bitcast.10, bf16[1536,1536]{1,0:T(8,128)(2,1)} %w_uq_ref.1, bf16[8,128,512]{2,1,0:T(8,128)(2,1)} %w_uk_ref.1, ...), custom_call_target="tpu_custom_call" | custom-call | tf_op jit(solution)/shard_map/attend/pallas_call | solution.py:457
  111.6 0.0 copy-done
  111.7 1.4 %fusion = bf16[64,8,128]{2,0,1:T(8,128)(2,1)S(1)} fusion(bf16[8,512,128]{2,1,0:T(8,128)(2,1)S(1)} %copy-done, bf16[64,8,512]{2,1,0:T(8,128)(2,1)} %bitcast.8), kind=kOutput, calls=%fused_computation.1 | convolution fusion | flops 67174400 | bytes 1703936 | tf_op jit(solution)/shard_map/qhc,hcv->qhv/dot_general | solution.py:606
  113.1 0.1 copy.13
  113.3 18.7 %project.1 = bf16[4,7168]{1,0:T(4,128)(2,1)S(1)} custom-call(bf16[64,1024]{1,0:T(8,128)(2,1)S(1)} %reshape.12.rows_ref, bf16[1024,7168]{1,0:T(8,128)(2,1)} %w_ref.1), custom_call_target="tpu_custom_call" | custom-call | tf_op jit(solution)/shard_map/project/pallas_call | solution.py:568
  132.0 0.6 copy.18
  (3 shorter events, 0.1 us)
Async XLA Ops:
  0.0 111.6 %copy-start = (bf16[8,512,128]{2,1,0:T(8,128)(2,1)S(1)}, bf16[8,512,128]{2,1,0:T(8,128)(2,1)}, u32[]{:S(2)}) copy-start(bf16[8,512,128]{2,1,0:T(8,128)(2,1)} %param.14) | copy-start | bytes 3145732
